TPU v7x, 768 devices: a whole 4x8x12 slice. The times are simulated.
768 devices in a mesh: rows: 192 (over x, z_hi, y, core), cols: 4 (over z_lo).
Axes of the slice: x: 4, y: 8, z: 12 (z_hi: 3, z_lo: 4; z = z_hi * 4 + z_lo), core: 2. Of those that a mesh axis runs over, the one named last changes fastest.
Arguments:
- frames: bfloat16 [2, 64, 3072, 512], P(None, None, 'rows', 'cols'), may hold values from -6 to 6
- hidden_state: bfloat16 [64, 3072, 512], P(None, 'rows', 'cols'), may hold values from -1 to 1
- cell_state: float32 [64, 3072, 512], P(None, 'rows', 'cols'), may hold values from -6 to 6
- depth_kernel: float32 [128, 3, 3], replicated, may hold values from -3 to 3
- point_weight: bfloat16 [256, 128], replicated, may hold values from -0.5 to 0.5
- gate_bias: float32 [256], replicated, may hold values from -3 to 3
- mixing_weight: bfloat16 [192, 64], replicated, may hold values from -0.75 to 0.75
- query_gain: float32 [64], replicated, may hold values from 0.2 to 40
- output_weight: bfloat16 [64, 64], replicated, may hold values from -0.75 to 0.75
Outputs:
- hidden_final: bfloat16 [64, 3072, 512], P(None, 'rows', 'cols')
- cell_final: float32 [64, 3072, 512], P(None, 'rows', 'cols')
- attended: float32 [2, 64, 384, 64], P(None, None, 'rows', 'cols')
All inputs are finite; a program needn't handle non-finite values.
Results may differ from a plain program's by a relative error of at most 0.0065.
Values may be sent and summed in bfloat16 or wider, within the bound.
A program may use at most 128 MiB of HBM per device.

v0:
```python
import math

import jax
import jax.numpy as jnp
from jax import lax
from jax.sharding import PartitionSpec as P

LEADS = 2


def with_halo(cells, sides, width):
    for axis, dim in sides:
        count = lax.axis_size(axis)
        ends = count - 1
        head = lax.slice_in_dim(cells, 0, width, axis=dim)
        tail = lax.slice_in_dim(cells, cells.shape[dim] - width, cells.shape[dim], axis=dim)
        cells = jnp.concatenate(
            [
                lax.ppermute(tail, axis, [(i, (i + 1) % count) for i in range(ends)]),
                cells,
                lax.ppermute(head, axis, [((i + 1) % count, i) for i in range(ends)]),
            ],
            axis=dim,
        )
    return cells


def depthwise(portion, depth_kernel, row_count, col_count):
    summed = None
    for a in range(3):
        for b in range(3):
            addend = (
                depth_kernel[:, a, b][:, None, None]
                * portion[:, a : a + row_count, b : b + col_count]
            )
            summed = addend if summed is None else summed + addend
    return summed


def recurrence(gates, previous):
    channels = previous.shape[0]
    in_gate = gates[:channels]
    forget = gates[channels : 2 * channels]
    out_gate = gates[2 * channels : 3 * channels]
    candidate = gates[3 * channels :]
    memory = jax.nn.sigmoid(forget) * previous + jax.nn.sigmoid(in_gate) * jnp.tanh(candidate)
    hidden = (jax.nn.sigmoid(out_gate) * jnp.tanh(memory)).astype(jnp.bfloat16)
    return (hidden, memory)


def normalize(vectors, axis):
    return vectors * lax.rsqrt(jnp.mean(vectors * vectors, axis=axis, keepdims=True) + 1e-06)


def gate_update(padded, memory, depth_kernel, point_weight, gate_bias):
    row_count, col_count = (memory.shape[1], memory.shape[2])
    spatial = depthwise(padded.astype(jnp.float32), depth_kernel, row_count, col_count).astype(
        jnp.bfloat16
    )
    gates = jnp.dot(
        point_weight, spatial.reshape(spatial.shape[0], -1), preferred_element_type=jnp.float32
    )
    gates = gates.reshape(-1, row_count, col_count) + gate_bias[:, None, None]
    return recurrence(gates, memory)


def attend(hidden, mixing_weight, query_gain, output_weight):
    channels, row_count, col_count = hidden.shape
    head_dim = query_gain.shape[0]
    pooled = (
        hidden.astype(jnp.float32)
        .reshape(channels, row_count // 8, 8, col_count // 8, 8)
        .mean(axis=(2, 4))
        .astype(jnp.bfloat16)
    )
    pool_rows, pool_cols = (pooled.shape[1], pooled.shape[2])
    flattened = pooled.reshape(channels, -1)
    query = jnp.dot(mixing_weight[:head_dim], flattened, preferred_element_type=jnp.float32)
    queries = (
        (normalize(query, 0) * query_gain[:, None])
        .astype(jnp.bfloat16)
        .reshape(head_dim, pool_rows, pool_cols)
    )
    inv_root = 1.0 / math.sqrt(head_dim)
    kv_weight = mixing_weight[head_dim:]
    band_rows = jnp.transpose(pooled, (1, 0, 2)).reshape(pool_rows, -1)
    portion = lax.all_gather(band_rows, "rows", axis=0, tiled=True)
    block_rows = portion.shape[0]
    shaped = portion.reshape(block_rows, channels, pool_cols)
    key_value = jnp.einsum("od,kdc->koc", kv_weight, shaped, preferred_element_type=jnp.float32)
    key_rows = normalize(key_value[:, :head_dim], 1).astype(jnp.bfloat16)
    running_max = jnp.full((pool_rows, pool_cols), -1e30, jnp.float32)
    scores = (
        jnp.einsum("dpc,kdc->pkc", queries, key_rows, preferred_element_type=jnp.float32) * inv_root
    )
    highest = jnp.maximum(running_max, jnp.max(scores, axis=1))
    weights = jnp.exp(scores - highest[:, None, :])
    mass_sum = jnp.sum(weights, axis=1)
    weighted = jnp.einsum(
        "pkc,kdc->dpc", weights, key_value[:, head_dim:].astype(jnp.bfloat16).astype(jnp.float32)
    )
    folded = (highest, mass_sum, weighted)
    running_max, mass_sum, weighted = folded
    mixed = (weighted / mass_sum[None]).astype(jnp.bfloat16)
    update = jnp.dot(output_weight, mixed.reshape(head_dim, -1), preferred_element_type=jnp.float32)
    return pooled.astype(jnp.float32) + update.reshape(channels, pool_rows, pool_cols)


def body(
    frames,
    hidden_state,
    cell_state,
    depth_kernel,
    point_weight,
    gate_bias,
    mixing_weight,
    query_gain,
    output_weight,
):
    hidden, memory = (hidden_state, cell_state)
    results = []
    for horizon in range(LEADS):
        stacked = jnp.concatenate([frames[horizon], hidden], axis=0)
        padded = with_halo(stacked, (("rows", 1), ("cols", 2)), 1)
        hidden, memory = gate_update(padded, memory, depth_kernel, point_weight, gate_bias)
        results.append(attend(hidden, mixing_weight, query_gain, output_weight))
    return (hidden, memory, jnp.stack(results))


def solution(mesh):
    in_specs = (
        P(None, None, "rows", "cols"),
        P(None, "rows", "cols"),
        P(None, "rows", "cols"),
        P(),
        P(),
        P(),
        P(),
        P(),
        P(),
    )
    out_specs = (P(None, "rows", "cols"), P(None, "rows", "cols"), P(None, None, "rows", "cols"))
    return jax.shard_map(body, mesh=mesh, in_specs=in_specs, out_specs=out_specs, check_vma=False)
```

profile of v0, /device:TPU:1, one launch (start us, length us, event | category | flops | bytes accessed | tf_op | source)
XLA Modules:
  0.0 767.2 jit_solution(14422212697684323849)
XLA Ops:
  0.6 1.3 copy.60
  3.5 12.4 %collective-permute-start.1 = (bf16[128,1,128]{0,2,1:T(8,128)(2,1)S(1)}, bf16[128,1,128]{0,2,1:T(8,128)(2,1)S(1)}, u32[]{:S(2)}, u32[]{:S(2)}) collective-permute-start(bf16[128,1,128]{0,2,1:T(8,128)(2,1)S(1)} %get-tuple-element.26), channel_id=1, source_target_pairs={{4,0},{8,4},{12,8},{16,12},{20,16},{24,20},{28,24},{32,28},{36,32}... | collective-permute-start | bytes 98312 | tf_op jit(solution)/shard_map/ppermute | solution.py:21
  15.9 1.9 collective-permute-start
  17.8 1.2 collective-permute-done
  19.7 1.3 collective-permute-start.3
  21.0 4.6 collective-permute-start.2
  27.0 1.2 maximum_convert_fusion
  30.0 2.1 fusion.46
  32.2 2.6 collective-permute-start.5
  34.8 3.9 collective-permute-start.4
  39.1 331.3 %all-gather = bf16[192,2,1024]{2,1,0:T(2,128)(2,1)S(1)} all-gather(bf16[1,2,1024]{2,1,0:T(2,128)(2,1)S(1)} %reshape.192), channel_id=1, replica_groups=mesh['rows'=192,'cols'=4] {'rows'}, dimensions={0}, use_global_device_ids=true | all-gather | bytes 790528 | tf_op jit(solution)/shard_map/all_gather | solution.py:87
  370.4 5.8 reshape.175
  376.2 9.8 %copy.63 = bf16[384,64,16]{0,1,2:T(8,128)(2,1)} copy(bf16[384,64,16]{2,1,0:T(8,128)(2,1)} %reshape.175) | data formatting | bytes 1572864 | tf_op jit(solution)/shard_map/reshape | solution.py:89
  386.0 1.8 convolution_bitcast_fusion.1
  389.1 1.3 collective-permute-start.7
  390.4 4.2 collective-permute-start.6
  398.0 2.2 fusion.47
  400.3 2.0 copy.72
  402.3 1.2 convert_reduce_fusion
  403.7 337.8 %all-gather.1 = bf16[192,2,1024]{2,1,0:T(2,128)(2,1)} all-gather(bf16[1,2,1024]{2,1,0:T(2,128)(2,1)S(1)} %reshape.194), channel_id=1, replica_groups=mesh['rows'=192,'cols'=4] {'rows'}, dimensions={0}, use_global_device_ids=true | all-gather | bytes 790528 | tf_op jit(solution)/shard_map/all_gather | solution.py:87
  741.5 7.8 %reshape.182 = bf16[384,64,16]{2,1,0:T(8,128)(2,1)} reshape(bf16[192,2,1024]{2,1,0:T(2,128)(2,1)} %all-gather.1) | data formatting | bytes 1572864 | tf_op jit(solution)/shard_map/reshape | solution.py:89
  749.3 9.8 %copy.68 = bf16[384,64,16]{0,1,2:T(8,128)(2,1)} copy(bf16[384,64,16]{2,1,0:T(8,128)(2,1)} %reshape.182) | data formatting | bytes 1572864 | tf_op jit(solution)/shard_map/reshape | solution.py:89
  759.1 1.8 convolution_bitcast_fusion
  763.6 2.4 copy.73
  (97 shorter events, 14.5 us)
Async XLA Ops:
  0.6 28.4 %copy-start = (bf16[256,128]{1,0:T(8,128)(2,1)S(1)}, bf16[256,128]{1,0:T(8,128)(2,1)}, u32[]{:S(2)}) copy-start(bf16[256,128]{1,0:T(8,128)(2,1)} %param.13) | copy-start | bytes 196612
  3.0 22.6 %copy-start.18 = (f32[128,3,3]{0,2,1:T(4,128)S(1)}, f32[128,3,3]{0,2,1:T(4,128)}, u32[]{:S(2)}) copy-start(f32[128,3,3]{0,2,1:T(4,128)} %param.12) | copy-start | bytes 13828
  3.0 23.2 %copy-start.6 = (f32[64,16,128]{2,1,0:T(8,128)S(1)}, f32[64,16,128]{2,1,0:T(8,128)}, u32[]{:S(2)}) copy-start(f32[64,16,128]{2,1,0:T(8,128)} %param.11) | copy-start | bytes 1572868
  3.5 14.4 %collective-permute-start.1 = (bf16[128,1,128]{0,2,1:T(8,128)(2,1)S(1)}, bf16[128,1,128]{0,2,1:T(8,128)(2,1)S(1)}, u32[]{:S(2)}, u32[]{:S(2)}) collective-permute-start(bf16[128,1,128]{0,2,1:T(8,128)(2,1)S(1)} %get-tuple-element.26), channel_id=1, source_target_pairs={{4,0},{8,4},{12,8},{16,12},{20,16},{24,20},{28,24},{32,28},{36,32}... | collective-permute-start | bytes 98312 | tf_op jit(solution)/shard_map/ppermute | solution.py:21
  15.9 3.1 collective-permute-start
  19.7 7.3 collective-permute-start.3
  21.0 6.0 collective-permute-start.2
  26.6 1.6 copy-start.9
  26.6 1.6 copy-start.10
  26.6 1.6 copy-start.11
  26.6 1.6 copy-start.12
  26.6 1.6 copy-start.13
  26.6 1.6 copy-start.14
  26.6 1.6 copy-start.15
  26.6 1.6 copy-start.16
  27.0 5.1 copy-start.3
  32.1 6.7 copy-start.1
  32.2 355.8 %collective-permute-start.5 = (bf16[128,1,128]{0,2,1:T(8,128)(2,1)S(1)}, bf16[128,1,128]{0,2,1:T(8,128)(2,1)S(1)}, u32[]{:S(2)}, u32[]{:S(2)}) collective-permute-start(bf16[128,1,128]{0,2,1:T(8,128)(2,1)S(1)} %get-tuple-element.24), channel_id=1, source_target_pairs={{4,0},{8,4},{12,8},{16,12},{20,16},{24,20},{28,24},{32,28},{36,32}... | collective-permute-start | bytes 98312 | tf_op jit(solution)/shard_map/ppermute | solution.py:21
  34.8 353.2 %collective-permute-start.4 = (bf16[128,1,128]{0,2,1:T(8,128)(2,1)S(1)}, bf16[128,1,128]{0,2,1:T(8,128)(2,1)S(1)}, u32[]{:S(2)}, u32[]{:S(2)}) collective-permute-start(bf16[128,1,128]{0,2,1:T(8,128)(2,1)S(1)} %get-tuple-element.23), channel_id=1, source_target_pairs={{0,4},{4,8},{8,12},{12,16},{16,20},{20,24},{24,28},{28,32},{32,36}... | collective-permute-start | bytes 98312 | tf_op jit(solution)/shard_map/ppermute | solution.py:19
  376.2 9.8 %copy-start.7 = (bf16[192,64]{0,1:T(8,128)(2,1)S(1)}, bf16[192,64]{0,1:T(8,128)(2,1)}, u32[]{:S(2)}) copy-start(bf16[192,64]{0,1:T(8,128)(2,1)} %param.15) | copy-start | bytes 73732
  389.1 5.7 collective-permute-start.7
  390.4 4.8 collective-permute-start.6
  396.8 1.2 copy-start.5
  763.0 3.2 copy-start.8
  (4 other events, 3.6 us)
where the time goes:
time: 768 us; the launch traced here: 767 us
  blocking collectives  669 us (87%)
  local copies, waits for them, and re-layouts  44.6 us (6%)
  starting transfers between devices  32.2 us (4%)
  other arithmetic  11.9 us (2%)
    all_gather x2, blocking collectives, attend(): portion = lax.all_gather(band_rows, 'rows', axis=0, tiled=True)  669 us
    reshape x4, local copies, waits for them, and re-layouts, attend(): shaped = portion.reshape(block_rows, channels, pool_cols)  33.2 us
    ppermute x4, starting transfers between devices, with_halo(): lax.ppermute(head, axis, [((i + 1) % count, i) for i in range(ends)])  17.6 us
  transfers between devices with their start and end apart: 8, of which 2 were waited for; matrix products, arithmetic and copies ran while one was open for 3% of the time, Pallas kernels for 0%

commit v1 on v0

v1 whole, which is shorter than its diff:
```python
import functools
import math

import jax
import jax.numpy as jnp
from jax import lax
from jax.experimental import pallas as pl
from jax.experimental.pallas import tpu as pltpu
from jax.sharding import PartitionSpec as P

LEADS = 2
MESH = pl.DeviceIdType.MESH


def with_halo(cells, sides, width):
    for axis, dim in sides:
        count = lax.axis_size(axis)
        ends = count - 1
        head = lax.slice_in_dim(cells, 0, width, axis=dim)
        tail = lax.slice_in_dim(cells, cells.shape[dim] - width, cells.shape[dim], axis=dim)
        cells = jnp.concatenate(
            [
                lax.ppermute(tail, axis, [(i, (i + 1) % count) for i in range(ends)]),
                cells,
                lax.ppermute(head, axis, [((i + 1) % count, i) for i in range(ends)]),
            ],
            axis=dim,
        )
    return cells


def depthwise(portion, depth_kernel, row_count, col_count):
    summed = None
    for a in range(3):
        for b in range(3):
            addend = (
                depth_kernel[:, a, b][:, None, None]
                * portion[:, a : a + row_count, b : b + col_count]
            )
            summed = addend if summed is None else summed + addend
    return summed


def recurrence(gates, previous):
    channels = previous.shape[0]
    in_gate = gates[:channels]
    forget = gates[channels : 2 * channels]
    out_gate = gates[2 * channels : 3 * channels]
    candidate = gates[3 * channels :]
    memory = jax.nn.sigmoid(forget) * previous + jax.nn.sigmoid(in_gate) * jnp.tanh(candidate)
    hidden = (jax.nn.sigmoid(out_gate) * jnp.tanh(memory)).astype(jnp.bfloat16)
    return (hidden, memory)


def gate_update(padded, memory, depth_kernel, point_weight, gate_bias):
    row_count, col_count = (memory.shape[1], memory.shape[2])
    spatial = depthwise(padded.astype(jnp.float32), depth_kernel, row_count, col_count).astype(
        jnp.bfloat16
    )
    gates = jnp.dot(
        point_weight, spatial.reshape(spatial.shape[0], -1), preferred_element_type=jnp.float32
    )
    gates = gates.reshape(-1, row_count, col_count) + gate_bias[:, None, None]
    return recurrence(gates, memory)


def lane_half(shape):
    return lax.broadcasted_iota(jnp.int32, shape, len(shape) - 1) < shape[-1] // 2


def half_norm(vectors, low):
    squares = vectors * vectors
    count = vectors.shape[-1] // 2
    first = jnp.sum(jnp.where(low, squares, 0.0), axis=-1, keepdims=True) / count
    second = jnp.sum(jnp.where(low, 0.0, squares), axis=-1, keepdims=True) / count
    return vectors * jnp.where(low, lax.rsqrt(first + 1e-06), lax.rsqrt(second + 1e-06))


def attend_column(own, every, qkv_weight, gain, out_weight):
    lanes = own.shape[-1]
    low = lane_half(own.shape)
    query = jnp.dot(own, qkv_weight[:, :lanes], preferred_element_type=jnp.float32)
    queries = half_norm(query, low) * gain
    turned = pltpu.roll(queries, lanes // 2, 1)
    stacked = jnp.concatenate(
        [
            jnp.where(low, queries, 0.0),
            jnp.where(low, turned, 0.0),
            jnp.where(low, 0.0, turned),
            jnp.where(low, 0.0, queries),
        ],
        axis=0,
    ).astype(jnp.bfloat16)
    key_value = jnp.dot(every, qkv_weight[:, lanes:], preferred_element_type=jnp.float32)
    keys = half_norm(key_value[:, :lanes], lane_half(every.shape)).astype(jnp.bfloat16)
    values = key_value[:, lanes:].astype(jnp.bfloat16)
    scores = lax.dot_general(
        stacked, keys, (((1,), (1,)), ((), ())), preferred_element_type=jnp.float32
    ) * (1.0 / math.sqrt(lanes // 2))
    count = own.shape[0]
    highest = jnp.max(scores, axis=1, keepdims=True)
    highest = jnp.maximum(highest[: 2 * count], highest[2 * count :])
    weights = jnp.exp(scores - jnp.concatenate([highest, highest], axis=0))
    mass = jnp.sum(weights, axis=1, keepdims=True)
    mass = mass[: 2 * count] + mass[2 * count :]
    weighted = jnp.dot(weights.astype(jnp.bfloat16), values, preferred_element_type=jnp.float32)
    swapped = pltpu.roll(weighted, lanes // 2, 1)
    mixed = jnp.where(
        low,
        (weighted[:count] + swapped[2 * count : 3 * count]) / mass[:count],
        (swapped[count : 2 * count] + weighted[3 * count :]) / mass[count:],
    )
    update = jnp.dot(mixed.astype(jnp.bfloat16), out_weight, preferred_element_type=jnp.float32)
    return own.astype(jnp.float32) + update


def attention_kernel(
    groups,
    members,
    pooled_ref,
    qkv_ref,
    gain_ref,
    out_weight_ref,
    out_ref,
    column,
    gathered,
    result,
    send_a,
    recv_a,
    send_b,
    recv_b,
    send_c,
    recv_c,
):
    me = lax.axis_index("rows")
    group, member = me // members, me % members

    def mate(step):
        return group * members + (member + step) % members

    def twin(step):
        return ((group + step) % groups) * members + member

    barrier = pltpu.get_barrier_semaphore()
    for step in range(1, members):
        pl.semaphore_signal(barrier, inc=1, device_id={"rows": mate(step)}, device_id_type=MESH)
    for step in range(1, groups):
        pl.semaphore_signal(barrier, inc=1, device_id={"rows": twin(step)}, device_id_type=MESH)
    pl.semaphore_wait(barrier, members + groups - 2)

    copies = []
    for step in range(1, members):
        target = (member + step) % members
        copies.append(
            pltpu.make_async_remote_copy(
                src_ref=pooled_ref.at[target],
                dst_ref=column.at[member],
                send_sem=send_a.at[step],
                recv_sem=recv_a.at[step],
                device_id={"rows": mate(step)},
                device_id_type=MESH,
            )
        )
        copies[-1].start()
    column[member] = pooled_ref[member]
    for copy in copies:
        copy.wait()
    for lead in range(LEADS):
        gathered[lead, group] = column[:, lead, :].astype(jnp.bfloat16)
    copies = []
    for step in range(1, groups):
        copies.append(
            pltpu.make_async_remote_copy(
                src_ref=gathered.at[:, group],
                dst_ref=gathered.at[:, group],
                send_sem=send_b.at[step],
                recv_sem=recv_b.at[step],
                device_id={"rows": twin(step)},
                device_id_type=MESH,
            )
        )
        copies[-1].start()
    for copy in copies:
        copy.wait()
    for lead in range(LEADS):
        result[:, lead, :] = attend_column(
            gathered[lead, group],
            gathered[lead].reshape(groups * members, -1),
            qkv_ref[...],
            gain_ref[...],
            out_weight_ref[...],
        )
    copies = []
    for step in range(1, members):
        target = (member + step) % members
        copies.append(
            pltpu.make_async_remote_copy(
                src_ref=result.at[target],
                dst_ref=out_ref.at[member],
                send_sem=send_c.at[step],
                recv_sem=recv_c.at[step],
                device_id={"rows": mate(step)},
                device_id_type=MESH,
            )
        )
        copies[-1].start()
    out_ref[member] = result[member]
    for copy in copies:
        copy.wait()


def twice(weight):
    zeros = jnp.zeros_like(weight)
    return jnp.concatenate(
        [jnp.concatenate([weight, zeros], axis=1), jnp.concatenate([zeros, weight], axis=1)], axis=0
    )


def pool(hidden):
    channels, row_count, col_count = hidden.shape
    return (
        hidden.astype(jnp.float32)
        .reshape(channels, row_count // 8, 8, col_count // 8, 8)
        .mean(axis=(2, 4))
        .astype(jnp.bfloat16)
    )


def attend(pooled, mixing_weight, query_gain, output_weight):
    leads, channels, pool_rows, members = pooled.shape
    groups = lax.axis_size("rows") // members
    head_dim = query_gain.shape[0]
    lanes = pool_rows * channels
    given = jnp.transpose(pooled, (3, 0, 2, 1)).reshape(members, leads, lanes).astype(jnp.float32)
    turned = mixing_weight.T
    qkv = jnp.concatenate(
        [twice(turned[:, k * head_dim : (k + 1) * head_dim]) for k in range(3)], axis=1
    )
    gain = jnp.concatenate([query_gain, query_gain])[None]
    dma = pltpu.SemaphoreType.DMA
    result = pl.pallas_call(
        functools.partial(attention_kernel, groups, members),
        out_shape=jax.ShapeDtypeStruct((members, leads, lanes), jnp.float32),
        in_specs=[pl.BlockSpec(memory_space=pltpu.VMEM)] * 4,
        out_specs=pl.BlockSpec(memory_space=pltpu.VMEM),
        scratch_shapes=[
            pltpu.VMEM((members, leads, lanes), jnp.float32),
            pltpu.VMEM((leads, groups, members, lanes), jnp.bfloat16),
            pltpu.VMEM((members, leads, lanes), jnp.float32),
            dma((members,)),
            dma((members,)),
            dma((groups,)),
            dma((groups,)),
            dma((members,)),
            dma((members,)),
        ],
        compiler_params=pltpu.CompilerParams(collective_id=0, has_side_effects=True),
    )(given, qkv, gain, twice(output_weight.T))
    return jnp.transpose(result.reshape(members, leads, pool_rows, channels), (1, 3, 2, 0))


def body(
    frames,
    hidden_state,
    cell_state,
    depth_kernel,
    point_weight,
    gate_bias,
    mixing_weight,
    query_gain,
    output_weight,
):
    hidden, memory = (hidden_state, cell_state)
    results = []
    for horizon in range(LEADS):
        stacked = jnp.concatenate([frames[horizon], hidden], axis=0)
        padded = with_halo(stacked, (("rows", 1), ("cols", 2)), 1)
        hidden, memory = gate_update(padded, memory, depth_kernel, point_weight, gate_bias)
        results.append(pool(hidden))
    attended = attend(jnp.stack(results), mixing_weight, query_gain, output_weight)
    return (hidden, memory, attended)


def solution(mesh):
    in_specs = (
        P(None, None, "rows", "cols"),
        P(None, "rows", "cols"),
        P(None, "rows", "cols"),
        P(),
        P(),
        P(),
        P(),
        P(),
        P(),
    )
    out_specs = (P(None, "rows", "cols"), P(None, "rows", "cols"), P(None, None, "rows", "cols"))
    return jax.shard_map(body, mesh=mesh, in_specs=in_specs, out_specs=out_specs, check_vma=False)
```

time: 768 us -> 96.5 us (0.13)
  blocking collectives: 669 us -> 0 us
  Pallas kernels: 0 us -> 46.4 us
  local copies, waits for them, and re-layouts: 44.6 us -> 7.2 us
    all_gather x2 -> x0, blocking collectives: 669 us -> none  [attend(): portion = lax.all_gather(band_rows, 'rows', axis=0, tiled=True)]
    pallas_call x0 -> x1, Pallas kernels: none -> 46.4 us  [attend(): pl.pallas_call(functools.partial(attention_kernel, groups, members), out_...]
    reshape x4 -> x2, local copies, waits for them, and re-layouts: 33.2 us -> 1.43 us  [attend(): result.reshape(members, leads, pool_rows, channels)]
  transfers between devices with their start and end apart: 8 -> 8, of which waited for: 2 -> 3; matrix products, arithmetic and copies ran while one was open for 3% -> 3% of each run, Pallas kernels for 0% -> 0%
where the time goes in v1:
time: 96.5 us; the launch traced here: 96 us
  Pallas kernels  46.4 us (48%)
  starting transfers between devices  25.9 us (27%)
  other arithmetic  7.87 us (8%)
  local copies, waits for them, and re-layouts  7.2 us (7%)
  waiting for transfers between devices  6.88 us (7%)
  between operations  0.97 us (1%)
    pallas_call x1, Pallas kernels, attend(): pl.pallas_call(functools.partial(attention_kernel, groups, members), out_...  46.4 us
    ppermute x4, starting transfers between devices, with_halo(): lax.ppermute(head, axis, [((i + 1) % count, i) for i in range(ends)])  14.3 us
    ppermute x4, starting transfers between devices, with_halo(): lax.ppermute(tail, axis, [(i, (i + 1) % count) for i in range(ends)])  11.6 us
    ppermute x4, waiting for transfers between devices, with_halo(): lax.ppermute(head, axis, [((i + 1) % count, i) for i in range(ends)])  6.87 us
    unnamed x25, local copies, waits for them, and re-layouts  3.85 us
    convert_element_type x2, other arithmetic, recurrence(): hidden = (jax.nn.sigmoid(out_gate) * jnp.tanh(memory)).astype(jnp.bfloat16)  2.22 us
  transfers between devices with their start and end apart: 8, of which 3 were waited for; matrix products, arithmetic and copies ran while one was open for 3% of the time, Pallas kernels for 0%

profile of v1, /device:TPU:1, one launch (start us, length us, event | category | flops | bytes accessed | tf_op | source)
XLA Modules:
  0.0 96.0 jit_solution(8638290834848079865)
XLA Ops:
  0.7 1.1 %fusion.75 = (bf16[1,64,16,128]{3,2,1,0:T(8,128)(2,1)S(1)}, bf16[1,64,16,128]{3,2,1,0:T(8,128)(2,1)S(1)}) fusion(bf16[2,64,16,128]{3,2,1,0:T(8,128)(2,1)} %param.9), kind=kLoop, calls=%fused_computation.140 | loop fusion | bytes 1048576 | tf_op jit(solution)/shard_map/slice | solution.py:276
  2.6 4.7 %collective-permute-start = (bf16[128,1,128]{0,2,1:T(8,128)(2,1)S(1)}, bf16[128,1,128]{0,2,1:T(8,128)(2,1)S(1)}, u32[]{:S(2)}, u32[]{:S(2)}) collective-permute-start(bf16[128,1,128]{0,2,1:T(8,128)(2,1)S(1)} %get-tuple-element.19), channel_id=1, source_target_pairs={{0,4},{4,8},{8,12},{12,16},{16,20},{20,24},{24,28},{28,32},{32,36}... | collective-permute-start | bytes 98312 | tf_op jit(solution)/shard_map/ppermute | solution.py:23
  7.3 9.1 %collective-permute-start.1 = (bf16[128,1,128]{0,2,1:T(8,128)(2,1)S(1)}, bf16[128,1,128]{0,2,1:T(8,128)(2,1)S(1)}, u32[]{:S(2)}, u32[]{:S(2)}) collective-permute-start(bf16[128,1,128]{0,2,1:T(8,128)(2,1)S(1)} %get-tuple-element.20), channel_id=1, source_target_pairs={{4,0},{8,4},{12,8},{16,12},{20,16},{24,20},{28,24},{32,28},{36,32}... | collective-permute-start | bytes 98312 | tf_op jit(solution)/shard_map/ppermute | solution.py:25
  16.6 0.7 fusion.65.qkv_ref
  17.6 1.3 %collective-permute-start.2 = (bf16[128,18,1]{0,2,1:T(2,128)(2,1)S(1)}, bf16[128,18,1]{0,2,1:T(2,128)(2,1)S(1)}, u32[]{:S(2)}, u32[]{:S(2)}) collective-permute-start(bf16[128,18,1]{0,2,1:T(2,128)(2,1)S(1)} %get-tuple-element.15), channel_id=1, source_target_pairs={{0,1},{1,2},{2,3},{4,5},{5,6},{6,7},{8,9},{9,10},{10,11},{12,13},{... | collective-permute-start | bytes 13832 | tf_op jit(solution)/shard_map/ppermute | solution.py:23
  18.8 1.3 %collective-permute-start.3 = (bf16[128,18,1]{0,2,1:T(2,128)(2,1)S(1)}, bf16[128,18,1]{0,2,1:T(2,128)(2,1)S(1)}, u32[]{:S(2)}, u32[]{:S(2)}) collective-permute-start(bf16[128,18,1]{0,2,1:T(2,128)(2,1)S(1)} %get-tuple-element.16), channel_id=1, source_target_pairs={{1,0},{2,1},{3,2},{5,4},{6,5},{7,6},{9,8},{10,9},{11,10},{13,12},{... | collective-permute-start | bytes 13832 | tf_op jit(solution)/shard_map/ppermute | solution.py:25
  20.1 0.7 fusion.70.out_weight_ref
  21.6 1.7 %collective-permute-done.3 = bf16[128,18,1]{0,2,1:T(2,128)(2,1)S(1)} collective-permute-done((bf16[128,18,1]{0,2,1:T(2,128)(2,1)S(1)}, bf16[128,18,1]{0,2,1:T(2,128)(2,1)S(1)}, u32[]{:S(2)}, u32[]{:S(2)}) %collective-permute-start.3) | collective-permute-done | bytes 4640 | tf_op jit(solution)/shard_map/ppermute | solution.py:25
  23.7 0.8 fusion.36
  25.4 1.1 %fusion.44 = (bf16[64,16,128]{0,2,1:T(8,128)(2,1)S(1)}, f32[64,16,128]{0,2,1:T(8,128)S(1)}) fusion(f32[256,16,128]{0,2,1:T(8,128)S(1)} %broadcast_add_fusion.1, f32[64,16,128]{0,2,1:T(8,128)S(1)} %copy.29), kind=kLoop, calls=%fused_computation.74 | loop fusion | flops 1835008 | bytes 3407872 | tf_op jit(solution)/shard_map/convert_element_type | solution.py:51
  26.6 1.9 %collective-permute-start.4 = (bf16[128,1,128]{0,2,1:T(8,128)(2,1)S(1)}, bf16[128,1,128]{0,2,1:T(8,128)(2,1)S(1)}, u32[]{:S(2)}, u32[]{:S(2)}) collective-permute-start(bf16[128,1,128]{0,2,1:T(8,128)(2,1)S(1)} %get-tuple-element.17), channel_id=1, source_target_pairs={{0,4},{4,8},{8,12},{12,16},{16,20},{20,24},{24,28},{28,32},{32,36}... | collective-permute-start | bytes 98312 | tf_op jit(solution)/shard_map/ppermute | solution.py:23
  28.6 2.6 %collective-permute-start.5 = (bf16[128,1,128]{0,2,1:T(8,128)(2,1)S(1)}, bf16[128,1,128]{0,2,1:T(8,128)(2,1)S(1)}, u32[]{:S(2)}, u32[]{:S(2)}) collective-permute-start(bf16[128,1,128]{0,2,1:T(8,128)(2,1)S(1)} %get-tuple-element.18), channel_id=1, source_target_pairs={{4,0},{8,4},{12,8},{16,12},{20,16},{24,20},{28,24},{32,28},{36,32}... | collective-permute-start | bytes 98312 | tf_op jit(solution)/shard_map/ppermute | solution.py:25
  31.2 0.6 maximum_bitcast_fusion.gain_ref
  31.9 1.9 %collective-permute-done.5 = bf16[128,1,128]{0,2,1:T(8,128)(2,1)S(1)} collective-permute-done((bf16[128,1,128]{0,2,1:T(8,128)(2,1)S(1)}, bf16[128,1,128]{0,2,1:T(8,128)(2,1)S(1)}, u32[]{:S(2)}, u32[]{:S(2)}) %collective-permute-start.5) | collective-permute-done | bytes 32800 | tf_op jit(solution)/shard_map/ppermute | solution.py:25
  33.9 3.6 %collective-permute-start.6 = (bf16[128,18,1]{0,2,1:T(2,128)(2,1)S(1)}, bf16[128,18,1]{0,2,1:T(2,128)(2,1)S(1)}, u32[]{:S(2)}, u32[]{:S(2)}) collective-permute-start(bf16[128,18,1]{0,2,1:T(2,128)(2,1)S(1)} %get-tuple-element.13), channel_id=1, source_target_pairs={{0,1},{1,2},{2,3},{4,5},{5,6},{6,7},{8,9},{9,10},{10,11},{12,13},{... | collective-permute-start | bytes 13832 | tf_op jit(solution)/shard_map/ppermute | solution.py:23
  37.5 1.3 %collective-permute-start.7 = (bf16[128,18,1]{0,2,1:T(2,128)(2,1)S(1)}, bf16[128,18,1]{0,2,1:T(2,128)(2,1)S(1)}, u32[]{:S(2)}, u32[]{:S(2)}) collective-permute-start(bf16[128,18,1]{0,2,1:T(2,128)(2,1)S(1)} %get-tuple-element.14), channel_id=1, source_target_pairs={{1,0},{2,1},{3,2},{5,4},{6,5},{7,6},{9,8},{10,9},{11,10},{13,12},{... | collective-permute-start | bytes 13832 | tf_op jit(solution)/shard_map/ppermute | solution.py:25
  39.0 3.2 %collective-permute-done.7 = bf16[128,18,1]{0,2,1:T(2,128)(2,1)S(1)} collective-permute-done((bf16[128,18,1]{0,2,1:T(2,128)(2,1)S(1)}, bf16[128,18,1]{0,2,1:T(2,128)(2,1)S(1)}, u32[]{:S(2)}, u32[]{:S(2)}) %collective-permute-start.7) | collective-permute-done | bytes 4640 | tf_op jit(solution)/shard_map/ppermute | solution.py:25
  42.7 0.8 fusion.14
  44.1 1.1 %fusion.45 = (bf16[64,16,128]{0,2,1:T(8,128)(2,1)S(1)}, f32[64,16,128]{0,2,1:T(8,128)S(1)}) fusion(f32[256,16,128]{0,2,1:T(8,128)S(1)} %broadcast_add_fusion, f32[64,16,128]{0,2,1:T(8,128)S(1)} %get-tuple-element.12), kind=kLoop, calls=%fused_computation.75 | loop fusion | flops 1835008 | bytes 3407872 | tf_op jit(solution)/shard_map/convert_element_type | solution.py:51
  45.2 1.0 %copy.33 = bf16[64,16,128]{2,1,0:T(8,128)(2,1)} copy(bf16[64,16,128]{0,2,1:T(8,128)(2,1)S(1)} %get-tuple-element.9) | data formatting | bytes 524288
  46.4 0.7 reshape.76.pooled_ref
  47.1 46.4 %shard_map.112 = f32[16,2,128]{2,1,0:T(2,128)} custom-call(f32[16,2,128]{2,1,0:T(2,128)} %reshape.76.pooled_ref, bf16[128,384]{1,0:T(8,128)(2,1)} %fusion.65.qkv_ref, f32[1,128]{1,0:T(1,128)} %maximum_bitcast_fusion.gain_ref, bf16[128,128]{1,0:T(8,128)(2,1)} %fusion.70.out_weight_ref), custom_call_target="tpu_custom_call" | custom-call | tf_op jit(solution)/shard_map/pallas_call | solution.py:241
  93.5 0.8 reshape.71
  94.9 1.1 %copy.34 = f32[64,16,128]{2,1,0:T(8,128)} copy(f32[64,16,128]{0,2,1:T(8,128)S(1)} %get-tuple-element.10) | data formatting | bytes 1048576
  (47 shorter events, 5.4 us)
Async XLA Ops:
  0.6 23.8 %copy-start = (bf16[256,128]{1,0:T(8,128)(2,1)S(1)}, bf16[256,128]{1,0:T(8,128)(2,1)}, u32[]{:S(2)}) copy-start(bf16[256,128]{1,0:T(8,128)(2,1)} %param.13) | copy-start | bytes 196612
  0.6 1.5 %copy-start.2 = (bf16[64,16,128]{2,1,0:T(8,128)(2,1)S(1)}, bf16[64,16,128]{2,1,0:T(8,128)(2,1)}, u32[]{:S(2)}) copy-start(bf16[64,16,128]{2,1,0:T(8,128)(2,1)} %param.10) | copy-start | bytes 786436
  1.8 14.7 %copy-start.6 = (f32[128,3,3]{0,2,1:T(4,128)S(1)}, f32[128,3,3]{0,2,1:T(4,128)}, u32[]{:S(2)}) copy-start(f32[128,3,3]{0,2,1:T(4,128)} %param.12) | copy-start | bytes 13828
  1.8 14.7 %copy-start.3 = (bf16[192,64]{0,1:T(8,128)(2,1)S(1)}, bf16[192,64]{0,1:T(8,128)(2,1)}, u32[]{:S(2)}) copy-start(bf16[192,64]{0,1:T(8,128)(2,1)} %param.15) | copy-start | bytes 73732
  1.8 14.8 %copy-start.7 = (pred[128]{0:T(512)(128)(4,1)S(1)}, pred[128]{0:T(512)(128)(4,1)}, u32[]{:S(2)}) copy-start(pred[128]{0:T(512)(128)(4,1)} %constant.10.clone.1) | copy-start | bytes 388
  2.2 15.2 %copy-start.4 = (bf16[64,64]{1,0:T(8,128)(2,1)S(1)}, bf16[64,64]{1,0:T(8,128)(2,1)}, u32[]{:S(2)}) copy-start(bf16[64,64]{1,0:T(8,128)(2,1)} %param.17) | copy-start | bytes 24580
  2.5 18.3 %copy-start.1 = (f32[64,16,128]{2,1,0:T(8,128)S(1)}, f32[64,16,128]{2,1,0:T(8,128)}, u32[]{:S(2)}) copy-start(f32[64,16,128]{2,1,0:T(8,128)} %param.11) | copy-start | bytes 1572868
  2.6 14.8 %collective-permute-start = (bf16[128,1,128]{0,2,1:T(8,128)(2,1)S(1)}, bf16[128,1,128]{0,2,1:T(8,128)(2,1)S(1)}, u32[]{:S(2)}, u32[]{:S(2)}) collective-permute-start(bf16[128,1,128]{0,2,1:T(8,128)(2,1)S(1)} %get-tuple-element.19), channel_id=1, source_target_pairs={{0,4},{4,8},{8,12},{12,16},{16,20},{20,24},{24,28},{28,32},{32,36}... | collective-permute-start | bytes 98312 | tf_op jit(solution)/shard_map/ppermute | solution.py:23
  7.3 10.1 %collective-permute-start.1 = (bf16[128,1,128]{0,2,1:T(8,128)(2,1)S(1)}, bf16[128,1,128]{0,2,1:T(8,128)(2,1)S(1)}, u32[]{:S(2)}, u32[]{:S(2)}) collective-permute-start(bf16[128,1,128]{0,2,1:T(8,128)(2,1)S(1)} %get-tuple-element.20), channel_id=1, source_target_pairs={{4,0},{8,4},{12,8},{16,12},{20,16},{24,20},{28,24},{32,28},{36,32}... | collective-permute-start | bytes 98312 | tf_op jit(solution)/shard_map/ppermute | solution.py:25
  17.6 4.0 %collective-permute-start.2 = (bf16[128,18,1]{0,2,1:T(2,128)(2,1)S(1)}, bf16[128,18,1]{0,2,1:T(2,128)(2,1)S(1)}, u32[]{:S(2)}, u32[]{:S(2)}) collective-permute-start(bf16[128,18,1]{0,2,1:T(2,128)(2,1)S(1)} %get-tuple-element.15), channel_id=1, source_target_pairs={{0,1},{1,2},{2,3},{4,5},{5,6},{6,7},{8,9},{9,10},{10,11},{12,13},{... | collective-permute-start | bytes 13832 | tf_op jit(solution)/shard_map/ppermute | solution.py:23
  18.8 4.4 %collective-permute-start.3 = (bf16[128,18,1]{0,2,1:T(2,128)(2,1)S(1)}, bf16[128,18,1]{0,2,1:T(2,128)(2,1)S(1)}, u32[]{:S(2)}, u32[]{:S(2)}) collective-permute-start(bf16[128,18,1]{0,2,1:T(2,128)(2,1)S(1)} %get-tuple-element.16), channel_id=1, source_target_pairs={{1,0},{2,1},{3,2},{5,4},{6,5},{7,6},{9,8},{10,9},{11,10},{13,12},{... | collective-permute-start | bytes 13832 | tf_op jit(solution)/shard_map/ppermute | solution.py:25
  24.5 0.7 copy-start.5
  25.4 5.8 %copy-start.8 = (f32[64]{0:T(128)S(1)}, f32[64]{0:T(128)}, u32[]{:S(2)}) copy-start(f32[64]{0:T(128)} %param.16) | copy-start | bytes 772
  26.6 5.2 %collective-permute-start.4 = (bf16[128,1,128]{0,2,1:T(8,128)(2,1)S(1)}, bf16[128,1,128]{0,2,1:T(8,128)(2,1)S(1)}, u32[]{:S(2)}, u32[]{:S(2)}) collective-permute-start(bf16[128,1,128]{0,2,1:T(8,128)(2,1)S(1)} %get-tuple-element.17), channel_id=1, source_target_pairs={{0,4},{4,8},{8,12},{12,16},{16,20},{20,24},{24,28},{28,32},{32,36}... | collective-permute-start | bytes 98312 | tf_op jit(solution)/shard_map/ppermute | solution.py:23
  28.6 5.2 %collective-permute-start.5 = (bf16[128,1,128]{0,2,1:T(8,128)(2,1)S(1)}, bf16[128,1,128]{0,2,1:T(8,128)(2,1)S(1)}, u32[]{:S(2)}, u32[]{:S(2)}) collective-permute-start(bf16[128,1,128]{0,2,1:T(8,128)(2,1)S(1)} %get-tuple-element.18), channel_id=1, source_target_pairs={{4,0},{8,4},{12,8},{16,12},{20,16},{24,20},{28,24},{32,28},{36,32}... | collective-permute-start | bytes 98312 | tf_op jit(solution)/shard_map/ppermute | solution.py:25
  33.9 5.1 %collective-permute-start.6 = (bf16[128,18,1]{0,2,1:T(2,128)(2,1)S(1)}, bf16[128,18,1]{0,2,1:T(2,128)(2,1)S(1)}, u32[]{:S(2)}, u32[]{:S(2)}) collective-permute-start(bf16[128,18,1]{0,2,1:T(2,128)(2,1)S(1)} %get-tuple-element.13), channel_id=1, source_target_pairs={{0,1},{1,2},{2,3},{4,5},{5,6},{6,7},{8,9},{9,10},{10,11},{12,13},{... | collective-permute-start | bytes 13832 | tf_op jit(solution)/shard_map/ppermute | solution.py:23
  37.5 4.7 %collective-permute-start.7 = (bf16[128,18,1]{0,2,1:T(2,128)(2,1)S(1)}, bf16[128,18,1]{0,2,1:T(2,128)(2,1)S(1)}, u32[]{:S(2)}, u32[]{:S(2)}) collective-permute-start(bf16[128,18,1]{0,2,1:T(2,128)(2,1)S(1)} %get-tuple-element.14), channel_id=1, source_target_pairs={{1,0},{2,1},{3,2},{5,4},{6,5},{7,6},{9,8},{10,9},{11,10},{13,12},{... | collective-permute-start | bytes 13832 | tf_op jit(solution)/shard_map/ppermute | solution.py:25

commit v2 on v0

v2 whole, which is shorter than its diff:
```python
import functools
import math

import jax
import jax.numpy as jnp
import numpy as np
from jax import lax
from jax.experimental import pallas as pl
from jax.experimental.pallas import tpu as pltpu
from jax.sharding import PartitionSpec as P

LEADS = 2
POOL = 8
MESH = pl.DeviceIdType.MESH
F32 = jnp.float32
BF16 = jnp.bfloat16
ROW_WAYS = (-1, 1)
EDGE_WAYS = tuple((dr, dc) for dr in (-1, 0, 1) for dc in (-1, 1))


def dot(left, right):
    return jnp.dot(left, right, preferred_element_type=F32)


def dot_t(left, right):
    return lax.dot_general(left, right, (((1,), (1,)), ((), ())), preferred_element_type=F32)


def lane_half(shape):
    return lax.broadcasted_iota(jnp.int32, shape, len(shape) - 1) < shape[-1] // 2


def half_norm(vectors, low):
    squares = vectors * vectors
    count = vectors.shape[-1] // 2
    first = jnp.sum(jnp.where(low, squares, 0.0), axis=-1, keepdims=True) / count
    second = jnp.sum(jnp.where(low, 0.0, squares), axis=-1, keepdims=True) / count
    return vectors * jnp.where(low, lax.rsqrt(first + 1e-06), lax.rsqrt(second + 1e-06))


def twice(weight):
    wide = jnp.concatenate([weight, weight], axis=1)
    low = lane_half(wide.shape)
    return jnp.concatenate([jnp.where(low, wide, 0.0), jnp.where(low, 0.0, wide)], axis=0)


def attend_column(own, every, mix_ref, gain, out_weight):
    lanes = own.shape[-1]
    low = lane_half(own.shape)
    queries = half_norm(dot_t(own, mix_ref[0]), low) * gain
    turned = pltpu.roll(queries, lanes // 2, 1)
    stacked = jnp.concatenate(
        [
            jnp.where(low, queries, 0.0),
            jnp.where(low, turned, 0.0),
            jnp.where(low, 0.0, turned),
            jnp.where(low, 0.0, queries),
        ],
        axis=0,
    ).astype(BF16)
    keys = half_norm(dot_t(every, mix_ref[1]), lane_half(every.shape)).astype(BF16)
    values = dot_t(every, mix_ref[2]).astype(BF16)
    scores = dot_t(stacked, keys) * (1.0 / math.sqrt(lanes // 2))
    count = own.shape[0]
    highest = jnp.max(scores, axis=1, keepdims=True)
    highest = jnp.maximum(highest[: 2 * count], highest[2 * count :])
    weights = jnp.exp(scores - jnp.concatenate([highest, highest], axis=0))
    mass = jnp.sum(weights, axis=1, keepdims=True)
    mass = mass[: 2 * count] + mass[2 * count :]
    weighted = dot(weights.astype(BF16), values)
    swapped = pltpu.roll(weighted, lanes // 2, 1)
    mixed = jnp.where(
        low,
        (weighted[:count] + swapped[2 * count : 3 * count]) / mass[:count],
        (swapped[count : 2 * count] + weighted[3 * count :]) / mass[count:],
    )
    return own.astype(F32) + dot_t(mixed.astype(BF16), out_weight)


def depthwise(x_ref, taps_ref, spatial_ref, blocks, bands):
    cols = x_ref.shape[2]

    def block(index, carry):
        lo = pl.multiple_of(index * 16, 16)
        taps = [taps_ref[k, pl.ds(lo, 16), :][None] for k in range(9)]
        for start, count in bands:
            rows = x_ref[start : start + count + 2, pl.ds(lo, 16), :]
            left, middle, right = (
                taps[b] * rows[:count]
                + taps[3 + b] * rows[1 : count + 1]
                + taps[6 + b] * rows[2 : count + 2]
                for b in range(3)
            )
            lane = lax.broadcasted_iota(jnp.int32, (count * 16, cols), 1)
            left = pltpu.roll(left.reshape(count * 16, cols), 1, 1)
            right = pltpu.roll(right.reshape(count * 16, cols), cols - 1, 1)
            total = (
                jnp.where(lane == 0, 0.0, left)
                + middle.reshape(count * 16, cols)
                + jnp.where(lane == cols - 1, 0.0, right)
            ).astype(BF16)
            for j in range(count):
                row = start + j
                spatial_ref[row // 2, pl.ds(lo, 16), (row % 2) * cols : (row % 2 + 1) * cols] = (
                    total[j * 16 : (j + 1) * 16]
                )
        return carry

    lax.fori_loop(blocks[0], blocks[1], block, None)


def halo_column(frame_tiles, hidden_tiles, way, masks, taps_t, pad_ref):
    seen, above, below = masks
    first = 8 if way == 1 else 0
    slot = {dr: EDGE_WAYS.index((dr, way)) for dr in (-1, 0, 1)}

    def part(dr):
        frame = frame_tiles(slot[dr]).astype(F32)[first : first + 8]
        hidden = hidden_tiles(slot[dr]).astype(F32)[first : first + 8]
        low = lane_half(frame.shape)
        half = frame.shape[1] // 2
        upper = jnp.where(low, frame, pltpu.roll(hidden, half, 1))
        lower = jnp.where(low, pltpu.roll(frame, half, 1), hidden)
        return jnp.where(seen, upper, 0.0), jnp.where(seen, lower, 0.0)

    upper, lower = part(0)
    pad_ref[0:8] = jnp.where(above, part(1)[1], 0.0)
    pad_ref[8:16] = upper
    pad_ref[16:24] = lower
    pad_ref[24:32] = jnp.where(below, part(-1)[0], 0.0)
    b = 0 if way == 1 else 2
    return sum(taps_t[3 * a + b] * pad_ref[7 + a : 23 + a] for a in range(3))


def kernel(
    n_rows,
    n_cols,
    groups,
    members,
    frames_ref,
    hidden_ref,
    cell_ref,
    spread_ref,
    pick_ref,
    depth_ref,
    point_ref,
    bias_ref,
    mixing_ref,
    gain_ref,
    output_ref,
    hidden_out,
    cell_out,
    attended_out,
    frames_in,
    hidden_in,
    cell_now,
    plain,
    x0,
    x1,
    taps,
    spatial0,
    spatial1,
    weight,
    stacked,
    row_out0,
    row_in0,
    edge_out0,
    edge_in0,
    row_out1,
    row_in1,
    edge_out1,
    edge_in1,
    pad,
    mix,
    out_mix,
    given,
    column,
    gathered,
    result,
    returned,
    local_sem,
    send_row,
    recv_row,
    send_edge,
    recv_edge,
    send_a,
    recv_a,
    send_b,
    recv_b,
    send_c,
    recv_c,
):
    row, col = lax.axis_index("rows"), lax.axis_index("cols")
    group, member = row // members, row % members
    channels = hidden_in.shape[0] // 16
    both = 2 * channels
    cols = hidden_in.shape[1]

    def near(dr, dc):
        return ((row + dr + n_rows) % n_rows, (col + dc + n_cols) % n_cols)

    def mate(step):
        return (group * members + (member + step) % members, col)

    def twin(step):
        return (((group + step) % groups) * members + member, col)

    loads = [
        pltpu.make_async_copy(frames_ref.at[0], frames_in.at[0], local_sem.at[0]),
        pltpu.make_async_copy(hidden_ref, hidden_in, local_sem.at[1]),
        pltpu.make_async_copy(frames_ref.at[1], frames_in.at[1], local_sem.at[2]),
        pltpu.make_async_copy(cell_ref, cell_now, local_sem.at[3]),
        pltpu.make_async_copy(spread_ref, spatial0.at[:, both:], local_sem.at[4]),
        pltpu.make_async_copy(spread_ref, spatial1.at[:, both:], local_sem.at[5]),
    ]
    for load in loads:
        load.start()

    barrier = pltpu.get_barrier_semaphore()
    peers = [near(dr, 0) for dr in ROW_WAYS] + [near(dr, dc) for dr, dc in EDGE_WAYS]
    peers += [twin(step) for step in range(1, groups)] + [mate(step) for step in range(1, members)]
    for peer in peers:
        pl.semaphore_signal(barrier, inc=1, device_id=peer, device_id_type=MESH)

    pick_edges = pick_ref[16:, :]
    for k, (source, load) in enumerate(
        ((frames_in.at[0], loads[0]), (hidden_in, loads[1]), (frames_in.at[1], loads[2]))
    ):
        load.wait()
        plain[...] = source[...].astype(F32)
        target, base = ((x0, 0), (x0, channels), (x1, 0))[k]
        for r in range(16):
            plane = plain[pl.ds(r, channels, stride=16), :]
            target[r + 1, base : base + channels, :] = plane
            low = plane.astype(BF16)
            stacked[
                (r // 8) * channels : (r // 8 + 1) * channels, (r % 8) * cols : (r % 8 + 1) * cols
            ] = low
            if r in (0, 15):
                row_out0[r // 15, k * channels : (k + 1) * channels, :] = low
        edge_out0[k] = dot_t(pick_edges, stacked[...]).astype(BF16)

    pl.semaphore_wait(barrier, len(peers))
    sends = []

    def send(source, target, send_sem, recv_sem, device):
        copy = pltpu.make_async_remote_copy(
            src_ref=source,
            dst_ref=target,
            send_sem=send_sem,
            recv_sem=recv_sem,
            device_id=device,
            device_id_type=MESH,
        )
        copy.start()
        sends.append(copy)
        return copy

    def send_halo(step, row_out, row_in, edge_out, edge_in):
        copies = []
        for k, dr in enumerate(ROW_WAYS):
            copies.append(
                send(
                    row_out.at[k],
                    row_in.at[k],
                    send_row.at[step, k],
                    recv_row.at[step, k],
                    near(dr, 0),
                )
            )
        for k, (dr, dc) in enumerate(EDGE_WAYS):
            copies.append(
                send(
                    edge_out,
                    edge_in.at[k],
                    send_edge.at[step, k],
                    recv_edge.at[step, k],
                    near(dr, dc),
                )
            )
        return copies

    halo0 = send_halo(0, row_out0, row_in0, edge_out0, edge_in0)

    depth = depth_ref[...]
    for k in range(9):
        taps[k] = jnp.broadcast_to(depth[:, k : k + 1], (both, cols))
    taps_t = {k: jnp.transpose(taps[k])[0:1] for k in range(9) if k % 3 != 1}
    lane = lax.broadcasted_iota(jnp.int32, (4 * channels, cols), 1)
    sublane = lax.broadcasted_iota(jnp.int32, (4 * channels, cols), 0)
    halve = jnp.where(sublane < 3 * channels, 0.5, 1.0)
    bias = jnp.transpose(jnp.broadcast_to(bias_ref[...], (cols, 4 * channels))) * halve
    weight[:, :both] = (point_ref[...].astype(F32) * halve).astype(BF16)
    for part in range(3):
        rounded = bias.astype(BF16).astype(F32)
        bias_lanes = rounded if part == 0 else jnp.where(lane == 64 + part, rounded, bias_lanes)
        bias = bias - rounded
    bias_lanes = jnp.where(lane < 67, bias_lanes, 0.0)
    for k in range(3):
        mix[k] = twice(mixing_ref[k * channels : (k + 1) * channels, :].astype(F32)).astype(BF16)
    out_mix[...] = twice(output_ref[...].astype(F32)).astype(BF16)
    gain = jnp.concatenate([gain_ref[...], gain_ref[...]], axis=1)

    above, below = row > 0, row < n_rows - 1
    interior, rim = ((1, 4), (5, 4), (9, 4), (13, 2)), ((0, 1), (15, 1))
    whole = channels // 16
    depthwise(x0, taps, spatial0, (0, 2 * whole), interior)
    depthwise(x1, taps, spatial1, (0, whole), interior)

    def fill_rows(x_ref, base, row_in, offset):
        x_ref[0, base : base + channels, :] = jnp.where(
            above, row_in[1, offset : offset + channels, :].astype(F32), 0.0
        )
        x_ref[17, base : base + channels, :] = jnp.where(
            below, row_in[0, offset : offset + channels, :].astype(F32), 0.0
        )

    def extend(frame_tiles, hidden_tiles):
        left = halo_column(frame_tiles, hidden_tiles, 1, (col > 0, above, below), taps_t, pad)
        right = halo_column(
            frame_tiles, hidden_tiles, -1, (col < n_cols - 1, above, below), taps_t, pad
        )
        rest = jnp.zeros((cols - 64, both), F32)
        added = jnp.concatenate([left, right, left, right, rest], axis=0).astype(BF16)
        lifted = dot_t(weight[:, :both], added)
        rounded = lifted.astype(BF16).astype(F32)
        weight[:, both:] = jnp.where(
            lane < 32, rounded, jnp.where(lane < 64, lifted - rounded, bias_lanes)
        ).astype(BF16)

    def update(step, spatial):
        for pair in range(8):
            gates = dot(weight[...], spatial[pair])
            for j in range(2):
                r = 2 * pair + j
                in_gate, forget, out_gate, candidate = (
                    jnp.tanh(gates[k * channels : (k + 1) * channels, j * cols : (j + 1) * cols])
                    for k in range(4)
                )
                place = pl.ds(r, channels, stride=16)
                memory = (0.5 * forget + 0.5) * cell_now[place, :] + (
                    0.5 * in_gate + 0.5
                ) * candidate
                cell_now[place, :] = memory
                hidden = (0.5 * out_gate + 0.5) * jnp.tanh(memory)
                low = hidden.astype(BF16)
                stacked[
                    (r // 8) * channels : (r // 8 + 1) * channels,
                    (r % 8) * cols : (r % 8 + 1) * cols,
                ] = low
                if step == 0:
                    x1[r + 1, channels:both, :] = low.astype(F32)
                    if r in (0, 15):
                        row_out1[r // 15] = low
                else:
                    plain[place, :] = hidden

    def share(lead, pooled):
        given[lead, :, 0, :] = pooled.astype(BF16).astype(F32)
        column[lead, member] = given[lead, member]
        copies = []
        for step in range(1, members):
            copies.append(
                send(
                    given.at[lead, (member + step) % members],
                    column.at[lead, member],
                    send_a.at[lead, step],
                    recv_a.at[lead, step],
                    mate(step),
                )
            )
        return copies

    def gather(lead, copies):
        for copy in copies:
            copy.wait_recv()
        gathered[lead, group] = column[lead, :, 0, :].astype(BF16)
        copies = []
        for step in range(1, groups):
            copies.append(
                send(
                    gathered.at[lead, group],
                    gathered.at[lead, group],
                    send_b.at[lead, step],
                    recv_b.at[lead, step],
                    twin(step),
                )
            )
        return copies

    def attend(lead, copies):
        for copy in copies:
            copy.wait_recv()
        result[lead, :, 0, :] = attend_column(
            gathered[lead, group],
            gathered[lead].reshape(groups * members, both),
            mix,
            gain,
            out_mix[...],
        )
        returned[lead, member] = result[lead, member]
        copies = []
        for step in range(1, members):
            copies.append(
                send(
                    result.at[lead, (member + step) % members],
                    returned.at[lead, member],
                    send_c.at[lead, step],
                    recv_c.at[lead, step],
                    mate(step),
                )
            )
        return copies

    for copy in halo0:
        copy.wait_recv()
    fill_rows(x0, 0, row_in0, 0)
    fill_rows(x0, channels, row_in0, channels)
    depthwise(x0, taps, spatial0, (0, 2 * whole), rim)
    extend(lambda k: edge_in0[k, 0], lambda k: edge_in0[k, 1])
    for load in loads[3:]:
        load.wait()
    update(0, spatial0)
    picked = dot_t(pick_ref[...], stacked[...])
    edge_out1[...] = picked[16:].astype(BF16)
    halo1 = send_halo(1, row_out1, row_in1, edge_out1, edge_in1)
    shared0 = share(0, picked[:16])
    fill_rows(x1, 0, row_in0, both)
    depthwise(x1, taps, spatial1, (0, whole), rim)
    depthwise(x1, taps, spatial1, (whole, 2 * whole), interior)
    for copy in halo1:
        copy.wait_recv()
    fill_rows(x1, channels, row_in1, 0)
    depthwise(x1, taps, spatial1, (whole, 2 * whole), rim)
    extend(lambda k: edge_in0[k, 2], lambda k: edge_in1[k])
    gathered0 = gather(0, shared0)
    update(1, spatial1)
    picked = dot_t(pick_ref[:16, :], stacked[...])
    shared1 = share(1, picked)
    store_cell = pltpu.make_async_copy(cell_now, cell_out, local_sem.at[6])
    store_cell.start()
    hidden_in[...] = plain[...].astype(BF16)
    store_hidden = pltpu.make_async_copy(hidden_in, hidden_out, local_sem.at[7])
    store_hidden.start()
    returned0 = attend(0, gathered0)
    gathered1 = gather(1, shared1)
    returned1 = attend(1, gathered1)
    for lead, copies in enumerate((returned0, returned1)):
        for copy in copies:
            copy.wait_recv()
        attended_out[lead] = returned[lead, :, 0, :]
    store_cell.wait()
    store_hidden.wait()
    for copy in sends:
        copy.wait_send()


def picker(cols, members):
    pick = np.zeros((32, POOL, cols), np.float32)
    for k in range(members):
        pick[k, :, k * POOL : (k + 1) * POOL] = 1.0 / (POOL * POOL)
    for r in range(POOL):
        pick[16 + r, r, 0] = 1.0
        pick[24 + r, r, cols - 1] = 1.0
    return pick.reshape(32, POOL * cols)


def spreader(cols):
    spread = np.zeros((8, 128, 2, cols), np.float32)
    for pair in range(8):
        for j in range(2):
            r = 2 * pair + j
            for twin in (0, 32):
                spread[pair, twin + r, j, 0] = 1.0
                spread[pair, twin + 16 + r, j, cols - 1] = 1.0
    spread[:, 64:67] = 1.0
    return spread.reshape(8, 128, 2 * cols)


def body(
    frames,
    hidden_state,
    cell_state,
    depth_kernel,
    point_weight,
    gate_bias,
    mixing_weight,
    query_gain,
    output_weight,
):
    channels, row_count, cols = hidden_state.shape
    both = 2 * channels
    flat = channels * row_count
    n_rows, n_cols = lax.axis_size("rows"), lax.axis_size("cols")
    members = cols // POOL
    groups = n_rows // members
    any_space = pl.BlockSpec(memory_space=pl.ANY)
    vmem = pl.BlockSpec(memory_space=pltpu.VMEM)
    dma = pltpu.SemaphoreType.DMA
    hidden, cell, attended = pl.pallas_call(
        functools.partial(kernel, n_rows, n_cols, groups, members),
        out_shape=(
            jax.ShapeDtypeStruct((flat, cols), BF16),
            jax.ShapeDtypeStruct((flat, cols), F32),
            jax.ShapeDtypeStruct((LEADS, members, both), F32),
        ),
        in_specs=[any_space] * 4 + [vmem] * 7,
        out_specs=(any_space, any_space, vmem),
        scratch_shapes=[
            pltpu.VMEM((LEADS, flat, cols), BF16),
            pltpu.VMEM((flat, cols), BF16),
            pltpu.VMEM((flat, cols), F32),
            pltpu.VMEM((flat, cols), F32),
            pltpu.VMEM((row_count + 2, both, cols), F32),
            pltpu.VMEM((row_count + 2, both, cols), F32),
            pltpu.VMEM((9, both, cols), F32),
            pltpu.VMEM((8, 2 * both, 2 * cols), BF16),
            pltpu.VMEM((8, 2 * both, 2 * cols), BF16),
            pltpu.VMEM((4 * channels, 2 * both), BF16),
            pltpu.VMEM((both, POOL * cols), BF16),
            pltpu.VMEM((2, 3 * channels, cols), BF16),
            pltpu.VMEM((2, 3 * channels, cols), BF16),
            pltpu.VMEM((3, 16, both), BF16),
            pltpu.VMEM((6, 3, 16, both), BF16),
            pltpu.VMEM((2, channels, cols), BF16),
            pltpu.VMEM((2, channels, cols), BF16),
            pltpu.VMEM((16, both), BF16),
            pltpu.VMEM((6, 16, both), BF16),
            pltpu.VMEM((32, both), F32),
            pltpu.VMEM((3, both, both), BF16),
            pltpu.VMEM((both, both), BF16),
            pltpu.VMEM((LEADS, members, 1, both), F32),
            pltpu.VMEM((LEADS, members, 1, both), F32),
            pltpu.VMEM((LEADS, groups, members, both), BF16),
            pltpu.VMEM((LEADS, members, 1, both), F32),
            pltpu.VMEM((LEADS, members, 1, both), F32),
            dma((8,)),
            dma((2, 2)),
            dma((2, 2)),
            dma((2, 6)),
            dma((2, 6)),
            dma((LEADS, members)),
            dma((LEADS, members)),
            dma((LEADS, groups)),
            dma((LEADS, groups)),
            dma((LEADS, members)),
            dma((LEADS, members)),
        ],
        compiler_params=pltpu.CompilerParams(
            collective_id=0, has_side_effects=True, vmem_limit_bytes=40 * 2**20
        ),
    )(
        frames.reshape(LEADS, flat, cols),
        hidden_state.reshape(flat, cols),
        cell_state.reshape(flat, cols),
        jnp.asarray(spreader(cols), BF16),
        jnp.asarray(picker(cols, members), BF16),
        depth_kernel.reshape(both, 9),
        point_weight,
        gate_bias[None],
        mixing_weight,
        query_gain[None],
        output_weight,
    )
    attended = jnp.transpose(attended.reshape(LEADS, members, 2, channels), (0, 3, 2, 1))
    shape = (channels, row_count, cols)
    return (hidden.reshape(shape), cell.reshape(shape), attended)


def solution(mesh):
    in_specs = (
        P(None, None, "rows", "cols"),
        P(None, "rows", "cols"),
        P(None, "rows", "cols"),
        P(),
        P(),
        P(),
        P(),
        P(),
        P(),
    )
    out_specs = (P(None, "rows", "cols"), P(None, "rows", "cols"), P(None, None, "rows", "cols"))
    return jax.shard_map(body, mesh=mesh, in_specs=in_specs, out_specs=out_specs, check_vma=False)
```

time: 768 us -> 65.4 us (0.09)
  blocking collectives: 669 us -> 0 us
  Pallas kernels: 0 us -> 55.7 us
  local copies, waits for them, and re-layouts: 44.6 us -> 8.57 us
  starting transfers between devices: 32.2 us -> 0 us
  other arithmetic: 11.9 us -> 0 us
    all_gather x2 -> x0, blocking collectives: 669 us -> none  [attend(): portion = lax.all_gather(band_rows, 'rows', axis=0, tiled=True)]
    pallas_call x0 -> x1, Pallas kernels: none -> 55.7 us  [body(): pl.pallas_call(functools.partial(kernel, n_rows, n_cols, groups, members)...]
    reshape x4, local copies, waits for them, and re-layouts: 33.2 us -> 0.82 us  [the longest x2 0.7 us: body(): attended.reshape(LEADS, members, 2, channels)]
    ppermute x8 -> x0, starting transfers between devices: 32.2 us -> none  [the longest x4 17.6 us: with_halo(): lax.ppermute(head, axis, [((i + 1) % count, i) for i in range(ends)])]
    convert_element_type x13 -> x0, other arithmetic: 7.75 us -> none  [the longest x2 4.33 us: recurrence(): hidden = (jax.nn.sigmoid(out_gate) * jnp.tanh(memory)).astype(jnp.bfloat16)]
  transfers between devices with their start and end apart: 8 -> 0, of which waited for: 2 -> 0; matrix products, arithmetic and copies ran while one was open for 3% -> 0% of each run, Pallas kernels for 0% -> 0%
where the time goes in v2:
time: 65.4 us; the launch traced here: 65 us
  Pallas kernels  55.7 us (85%)
  local copies, waits for them, and re-layouts  8.57 us (13%)
  between operations  0.69 us (1%)
    pallas_call x1, Pallas kernels, body(): pl.pallas_call(functools.partial(kernel, n_rows, n_cols, groups, members)...  55.7 us
    unnamed x23, local copies, waits for them, and re-layouts  7.75 us

profile of v2, /device:TPU:1, one launch (start us, length us, event | category | flops | bytes accessed | tf_op | source)
XLA Modules:
  0.0 65.0 jit_solution(12146364389349248925)
XLA Ops:
  0.6 0.0 copy-start.9
  0.6 0.7 %copy-done.9 = f32[128,3,3]{0,2,1:T(4,128)S(1)} copy-done((f32[128,3,3]{0,2,1:T(4,128)S(1)}, f32[128,3,3]{0,2,1:T(4,128)}, u32[]{:S(2)}) %copy-start.9) | copy-done | bytes 4632
  1.3 0.0 copy-start.4
  1.3 0.0 copy-start.5
  1.3 0.9 %copy.18.mixing_ref = bf16[192,64]{1,0:T(8,128)(2,1)S(1)} copy(bf16[192,64]{0,1:T(8,128)(2,1)} %param.17) | data formatting | bytes 49152 | tf_op args[6]
  2.2 0.0 copy-start.6
  2.2 0.0 copy-start.7
  2.3 0.0 copy-start.8
  2.3 0.1 copy.17.depth_ref
  2.4 0.0 copy-done.4
  2.4 0.0 copy-done.5
  2.4 0.6 copy-done.6
  3.0 0.0 copy-done.7
  3.0 0.0 copy-done.8
  3.0 0.0 copy-start
  3.0 1.0 %copy-done = bf16[2,64,16,128]{3,2,1,0:T(8,128)(2,1)S(1)} copy-done((bf16[2,64,16,128]{3,2,1,0:T(8,128)(2,1)S(1)}, bf16[2,64,16,128]{3,2,1,0:T(8,128)(2,1)}, u32[]{:S(2)}) %copy-start) | copy-done | bytes 524312
  4.0 1.0 %copy-done.1 = f32[64,16,128]{2,1,0:T(8,128)S(1)} copy-done((f32[64,16,128]{2,1,0:T(8,128)S(1)}, f32[64,16,128]{2,1,0:T(8,128)}, u32[]{:S(2)}) %copy-start.1) | copy-done | bytes 524312
  5.1 1.0 %copy-done.2 = bf16[8,128,256]{2,1,0:T(8,128)(2,1)S(1)} copy-done((bf16[8,128,256]{2,1,0:T(8,128)(2,1)S(1)}, bf16[8,128,256]{2,1,0:T(8,128)(2,1)}, u32[]{:S(2)}) %copy-start.2) | copy-done | bytes 524312
  6.1 0.9 %copy-done.3 = bf16[64,16,128]{2,1,0:T(8,128)(2,1)S(1)} copy-done((bf16[64,16,128]{2,1,0:T(8,128)(2,1)S(1)}, bf16[64,16,128]{2,1,0:T(8,128)(2,1)}, u32[]{:S(2)}) %copy-start.3) | copy-done | bytes 262168
  7.1 55.7 %shard_map.130 = (bf16[1024,128]{1,0:T(8,128)(2,1)S(1)}, f32[1024,128]{1,0:T(8,128)S(1)}, f32[2,16,128]{2,1,0:T(8,128)S(1)}) custom-call(bf16[2,1024,128]{2,1,0:T(8,128)(2,1)S(1)} %bitcast.13, bf16[1024,128]{1,0:T(8,128)(2,1)S(1)} %bitcast.15, f32[1024,128]{1,0:T(8,128)S(1)} %bitcast.14, bf16[8,128,256]{2,1,0:T(8,128)(2,1)S(1)} %copy-done.2, ...), custom_call_target="tpu_custom_call" | custom-call | tf_op jit(solution)/shard_map/pallas_call | solution.py:500
  62.8 0.1 reshape.33
  62.9 0.6 copy.21
  63.5 0.7 %copy.24 = bf16[64,16,128]{2,1,0:T(8,128)(2,1)} copy(bf16[64,16,128]{2,1,0:T(8,128)(2,1)S(1)} %bitcast.16) | data formatting | bytes 524288
  64.2 0.8 %copy.25 = f32[64,16,128]{2,1,0:T(8,128)} copy(f32[64,16,128]{2,1,0:T(8,128)S(1)} %bitcast.12) | data formatting | bytes 1048576
  (4 shorter events, 0.0 us)
Async XLA Ops:
  0.6 0.7 %copy-start.9 = (f32[128,3,3]{0,2,1:T(4,128)S(1)}, f32[128,3,3]{0,2,1:T(4,128)}, u32[]{:S(2)}) copy-start(f32[128,3,3]{0,2,1:T(4,128)} %param.14) | copy-start | bytes 13828
  1.3 1.1 %copy-start.4 = (bf16[256,128]{1,0:T(8,128)(2,1)S(1)}, bf16[256,128]{1,0:T(8,128)(2,1)}, u32[]{:S(2)}) copy-start(bf16[256,128]{1,0:T(8,128)(2,1)} %point_ref.1) | copy-start | bytes 196612
  1.3 1.1 %copy-start.5 = (bf16[32,1024]{1,0:T(8,128)(2,1)S(1)}, bf16[32,1024]{1,0:T(8,128)(2,1)}, u32[]{:S(2)}) copy-start(bf16[32,1024]{1,0:T(8,128)(2,1)} %constant.5.clone.pick_ref) | copy-start | bytes 196612
  2.2 0.7 %copy-start.6 = (bf16[64,64]{1,0:T(8,128)(2,1)S(1)}, bf16[64,64]{1,0:T(8,128)(2,1)}, u32[]{:S(2)}) copy-start(bf16[64,64]{1,0:T(8,128)(2,1)} %output_ref.1) | copy-start | bytes 24580
  2.2 0.7 %copy-start.7 = (f32[256]{0:T(256)S(1)}, f32[256]{0:T(256)}, u32[]{:S(2)}) copy-start(f32[256]{0:T(256)} %param.16) | copy-start | bytes 3076
  2.3 0.7 %copy-start.8 = (f32[64]{0:T(128)S(1)}, f32[64]{0:T(128)}, u32[]{:S(2)}) copy-start(f32[64]{0:T(128)} %param.18) | copy-start | bytes 772
  3.0 1.0 %copy-start = (bf16[2,64,16,128]{3,2,1,0:T(8,128)(2,1)S(1)}, bf16[2,64,16,128]{3,2,1,0:T(8,128)(2,1)}, u32[]{:S(2)}) copy-start(bf16[2,64,16,128]{3,2,1,0:T(8,128)(2,1)} %param.11) | copy-start | bytes 1572868
  4.0 1.0 %copy-start.1 = (f32[64,16,128]{2,1,0:T(8,128)S(1)}, f32[64,16,128]{2,1,0:T(8,128)}, u32[]{:S(2)}) copy-start(f32[64,16,128]{2,1,0:T(8,128)} %param.13) | copy-start | bytes 1572868
  5.1 1.0 %copy-start.2 = (bf16[8,128,256]{2,1,0:T(8,128)(2,1)S(1)}, bf16[8,128,256]{2,1,0:T(8,128)(2,1)}, u32[]{:S(2)}) copy-start(bf16[8,128,256]{2,1,0:T(8,128)(2,1)} %constant.4.clone.spread_ref) | copy-start | bytes 1572868
  6.1 0.9 %copy-start.3 = (bf16[64,16,128]{2,1,0:T(8,128)(2,1)S(1)}, bf16[64,16,128]{2,1,0:T(8,128)(2,1)}, u32[]{:S(2)}) copy-start(bf16[64,16,128]{2,1,0:T(8,128)(2,1)} %param.12) | copy-start | bytes 786436

commit v3 on v2

--- a/solution.py
+++ b/solution.py
@@ -11,6 +11,7 @@
 
 LEADS = 2
 POOL = 8
+LINES = 4
 MESH = pl.DeviceIdType.MESH
 F32 = jnp.float32
 BF16 = jnp.bfloat16
@@ -62,6 +63,9 @@
     values = dot_t(every, mix_ref[2]).astype(BF16)
     scores = dot_t(stacked, keys) * (1.0 / math.sqrt(lanes // 2))
     count = own.shape[0]
+    query_column = lax.broadcasted_iota(jnp.int32, scores.shape, 0) // 8 % 2
+    key_column = lax.broadcasted_iota(jnp.int32, scores.shape, 1) // 8 % 2
+    scores = jnp.where(query_column == key_column, scores, -1e30)
     highest = jnp.max(scores, axis=1, keepdims=True)
     highest = jnp.maximum(highest[: 2 * count], highest[2 * count :])
     weights = jnp.exp(scores - jnp.concatenate([highest, highest], axis=0))
@@ -151,6 +155,13 @@
     hidden_out,
     cell_out,
     attended_out,
+    point_in,
+    depth_in,
+    bias_in,
+    mixing_in,
+    gain_in,
+    output_in,
+    pick_in,
     frames_in,
     hidden_in,
     cell_now,
@@ -191,7 +202,8 @@
     recv_c,
 ):
     row, col = lax.axis_index("rows"), lax.axis_index("cols")
-    group, member = row // members, row % members
+    core, group, line = row % 2, row // 2 % groups, row // (2 * groups)
+    member = line * 2 + core
     channels = hidden_in.shape[0] // 16
     both = 2 * channels
     cols = hidden_in.shape[1]
@@ -200,10 +212,11 @@
         return ((row + dr + n_rows) % n_rows, (col + dc + n_cols) % n_cols)
 
     def mate(step):
-        return (group * members + (member + step) % members, col)
+        target = (member + step) % members
+        return ((target // 2 * groups + group) * 2 + target % 2, col)
 
     def twin(step):
-        return (((group + step) % groups) * members + member, col)
+        return ((line * groups + (group + step) % groups) * 2 + core, col)
 
     loads = [
         pltpu.make_async_copy(frames_ref.at[0], frames_in.at[0], local_sem.at[0]),
@@ -213,16 +226,31 @@
         pltpu.make_async_copy(spread_ref, spatial0.at[:, both:], local_sem.at[4]),
         pltpu.make_async_copy(spread_ref, spatial1.at[:, both:], local_sem.at[5]),
     ]
-    for load in loads:
+    small = [
+        pltpu.make_async_copy(source, target, local_sem.at[8 + k])
+        for k, (source, target) in enumerate(
+            (
+                (pick_ref, pick_in),
+                (depth_ref, depth_in),
+                (point_ref, point_in),
+                (bias_ref, bias_in),
+                (mixing_ref, mixing_in),
+                (gain_ref, gain_in),
+                (output_ref, output_in),
+            )
+        )
+    ]
+    for load in loads[:1] + small[:1] + loads[1:] + small[1:]:
         load.start()
 
     barrier = pltpu.get_barrier_semaphore()
-    peers = [near(dr, 0) for dr in ROW_WAYS] + [near(dr, dc) for dr, dc in EDGE_WAYS]
+    peers = [near(dr, dc) for dr, dc in EDGE_WAYS] + [near(dr, 0) for dr in ROW_WAYS]
     peers += [twin(step) for step in range(1, groups)] + [mate(step) for step in range(1, members)]
     for peer in peers:
         pl.semaphore_signal(barrier, inc=1, device_id=peer, device_id_type=MESH)
 
-    pick_edges = pick_ref[16:, :]
+    small[0].wait()
+    pick_edges = pick_in[16:, :]
     for k, (source, load) in enumerate(
         ((frames_in.at[0], loads[0]), (hidden_in, loads[1]), (frames_in.at[1], loads[2]))
     ):
@@ -282,24 +310,27 @@
 
     halo0 = send_halo(0, row_out0, row_in0, edge_out0, edge_in0)
 
-    depth = depth_ref[...]
+    for load in small[1:]:
+        load.wait()
+    taps_t = [depth_in[k // 3, k % 3 : k % 3 + 1, :] for k in range(9)]
+    depth = jnp.transpose(jnp.concatenate(taps_t + [jnp.zeros((both - 9, both), F32)], axis=0))
     for k in range(9):
         taps[k] = jnp.broadcast_to(depth[:, k : k + 1], (both, cols))
-    taps_t = {k: jnp.transpose(taps[k])[0:1] for k in range(9) if k % 3 != 1}
     lane = lax.broadcasted_iota(jnp.int32, (4 * channels, cols), 1)
     sublane = lax.broadcasted_iota(jnp.int32, (4 * channels, cols), 0)
     halve = jnp.where(sublane < 3 * channels, 0.5, 1.0)
-    bias = jnp.transpose(jnp.broadcast_to(bias_ref[...], (cols, 4 * channels))) * halve
-    weight[:, :both] = (point_ref[...].astype(F32) * halve).astype(BF16)
+    bias = jnp.transpose(jnp.broadcast_to(bias_in[...], (cols, 4 * channels))) * halve
+    weight[:, :both] = (point_in[...].astype(F32) * halve).astype(BF16)
     for part in range(3):
         rounded = bias.astype(BF16).astype(F32)
         bias_lanes = rounded if part == 0 else jnp.where(lane == 64 + part, rounded, bias_lanes)
         bias = bias - rounded
     bias_lanes = jnp.where(lane < 67, bias_lanes, 0.0)
+    mixing = jnp.transpose(mixing_in[...].astype(F32))
     for k in range(3):
-        mix[k] = twice(mixing_ref[k * channels : (k + 1) * channels, :].astype(F32)).astype(BF16)
-    out_mix[...] = twice(output_ref[...].astype(F32)).astype(BF16)
-    gain = jnp.concatenate([gain_ref[...], gain_ref[...]], axis=1)
+        mix[k] = twice(mixing[k * channels : (k + 1) * channels]).astype(BF16)
+    out_mix[...] = twice(output_in[...].astype(F32)).astype(BF16)
+    gain = jnp.concatenate([gain_in[...], gain_in[...]], axis=1)
 
     above, below = row > 0, row < n_rows - 1
     interior, rim = ((1, 4), (5, 4), (9, 4), (13, 2)), ((0, 1), (15, 1))
@@ -356,7 +387,9 @@
                     plain[place, :] = hidden
 
     def share(lead, pooled):
-        given[lead, :, 0, :] = pooled.astype(BF16).astype(F32)
+        pooled = pooled.astype(BF16).astype(F32)
+        for k in range(members):
+            given[lead, k] = pooled[2 * k : 2 * k + 2]
         column[lead, member] = given[lead, member]
         copies = []
         for step in range(1, members):
@@ -374,7 +407,9 @@
     def gather(lead, copies):
         for copy in copies:
             copy.wait_recv()
-        gathered[lead, group] = column[lead, :, 0, :].astype(BF16)
+        gathered[lead, group] = jnp.concatenate(
+            [column[lead, :, k, :] for k in range(2)], axis=0
+        ).astype(BF16)
         copies = []
         for step in range(1, groups):
             copies.append(
@@ -391,13 +426,15 @@
     def attend(lead, copies):
         for copy in copies:
             copy.wait_recv()
-        result[lead, :, 0, :] = attend_column(
+        attended = attend_column(
             gathered[lead, group],
-            gathered[lead].reshape(groups * members, both),
+            gathered[lead].reshape(groups * 2 * members, both),
             mix,
             gain,
             out_mix[...],
         )
+        for k in range(2):
+            result[lead, :, k, :] = attended[k * members : (k + 1) * members]
         returned[lead, member] = result[lead, member]
         copies = []
         for step in range(1, members):
@@ -421,7 +458,7 @@
     for load in loads[3:]:
         load.wait()
     update(0, spatial0)
-    picked = dot_t(pick_ref[...], stacked[...])
+    picked = dot_t(pick_in[...], stacked[...])
     edge_out1[...] = picked[16:].astype(BF16)
     halo1 = send_halo(1, row_out1, row_in1, edge_out1, edge_in1)
     shared0 = share(0, picked[:16])
@@ -435,7 +472,7 @@
     extend(lambda k: edge_in0[k, 2], lambda k: edge_in1[k])
     gathered0 = gather(0, shared0)
     update(1, spatial1)
-    picked = dot_t(pick_ref[:16, :], stacked[...])
+    picked = dot_t(pick_in[:16, :], stacked[...])
     shared1 = share(1, picked)
     store_cell = pltpu.make_async_copy(cell_now, cell_out, local_sem.at[6])
     store_cell.start()
@@ -448,16 +485,18 @@
     for lead, copies in enumerate((returned0, returned1)):
         for copy in copies:
             copy.wait_recv()
-        attended_out[lead] = returned[lead, :, 0, :]
+        attended = jnp.concatenate([returned[lead, k] for k in range(members)], axis=0)
+        for k in range(2):
+            attended_out[lead, k] = attended[:, k * channels : (k + 1) * channels]
     store_cell.wait()
     store_hidden.wait()
     for copy in sends:
         copy.wait_send()
 
 
-def picker(cols, members):
+def picker(cols):
     pick = np.zeros((32, POOL, cols), np.float32)
-    for k in range(members):
+    for k in range(cols // POOL):
         pick[k, :, k * POOL : (k + 1) * POOL] = 1.0 / (POOL * POOL)
     for r in range(POOL):
         pick[16 + r, r, 0] = 1.0
@@ -492,8 +531,9 @@
     both = 2 * channels
     flat = channels * row_count
     n_rows, n_cols = lax.axis_size("rows"), lax.axis_size("cols")
-    members = cols // POOL
+    members = 2 * LINES
     groups = n_rows // members
+    hbm = pl.BlockSpec(memory_space=pltpu.HBM)
     any_space = pl.BlockSpec(memory_space=pl.ANY)
     vmem = pl.BlockSpec(memory_space=pltpu.VMEM)
     dma = pltpu.SemaphoreType.DMA
@@ -502,11 +542,18 @@
         out_shape=(
             jax.ShapeDtypeStruct((flat, cols), BF16),
             jax.ShapeDtypeStruct((flat, cols), F32),
-            jax.ShapeDtypeStruct((LEADS, members, both), F32),
+            jax.ShapeDtypeStruct((LEADS, 2, cols // POOL, channels), F32),
         ),
-        in_specs=[any_space] * 4 + [vmem] * 7,
+        in_specs=[hbm] * 11,
         out_specs=(any_space, any_space, vmem),
         scratch_shapes=[
+            pltpu.VMEM((4 * channels, both), BF16),
+            pltpu.VMEM((3, 3, both), F32),
+            pltpu.VMEM((1, 4 * channels), F32),
+            pltpu.VMEM((channels, 3 * channels), BF16),
+            pltpu.VMEM((1, channels), F32),
+            pltpu.VMEM((channels, channels), BF16),
+            pltpu.VMEM((32, POOL * cols), BF16),
             pltpu.VMEM((LEADS, flat, cols), BF16),
             pltpu.VMEM((flat, cols), BF16),
             pltpu.VMEM((flat, cols), F32),
@@ -529,12 +576,12 @@
             pltpu.VMEM((32, both), F32),
             pltpu.VMEM((3, both, both), BF16),
             pltpu.VMEM((both, both), BF16),
-            pltpu.VMEM((LEADS, members, 1, both), F32),
-            pltpu.VMEM((LEADS, members, 1, both), F32),
-            pltpu.VMEM((LEADS, groups, members, both), BF16),
-            pltpu.VMEM((LEADS, members, 1, both), F32),
-            pltpu.VMEM((LEADS, members, 1, both), F32),
-            dma((8,)),
+            pltpu.VMEM((LEADS, members, 2, both), F32),
+            pltpu.VMEM((LEADS, members, 2, both), F32),
+            pltpu.VMEM((LEADS, groups, 2 * members, both), BF16),
+            pltpu.VMEM((LEADS, members, 2, both), F32),
+            pltpu.VMEM((LEADS, members, 2, both), F32),
+            dma((15,)),
             dma((2, 2)),
             dma((2, 2)),
             dma((2, 6)),
@@ -547,22 +594,22 @@
             dma((LEADS, members)),
         ],
         compiler_params=pltpu.CompilerParams(
-            collective_id=0, has_side_effects=True, vmem_limit_bytes=40 * 2**20
+            collective_id=0, has_side_effects=True, vmem_limit_bytes=60 * 2**20
         ),
     )(
         frames.reshape(LEADS, flat, cols),
         hidden_state.reshape(flat, cols),
         cell_state.reshape(flat, cols),
         jnp.asarray(spreader(cols), BF16),
-        jnp.asarray(picker(cols, members), BF16),
-        depth_kernel.reshape(both, 9),
+        jnp.asarray(picker(cols), BF16),
+        jnp.transpose(depth_kernel, (1, 2, 0)),
         point_weight,
         gate_bias[None],
-        mixing_weight,
+        mixing_weight.T,
         query_gain[None],
         output_weight,
     )
-    attended = jnp.transpose(attended.reshape(LEADS, members, 2, channels), (0, 3, 2, 1))
+    attended = jnp.transpose(attended, (0, 3, 1, 2))
     shape = (channels, row_count, cols)
     return (hidden.reshape(shape), cell.reshape(shape), attended)
 

time: 65.4 us -> 65.3 us (level)
  Pallas kernels: 55.7 us -> 61.3 us
  local copies, waits for them, and re-layouts: 8.57 us -> 3.14 us
    pallas_call x1, Pallas kernels: 55.7 us -> 61.3 us  [body(): pl.pallas_call(functools.partial(kernel, n_rows, n_cols, groups, members)...]
    unnamed x23 -> x7, local copies, waits for them, and re-layouts: 7.75 us -> 3.14 us
    reshape x4 -> x0, local copies, waits for them, and re-layouts: 0.82 us -> none  [the longest x2 0.7 us: body(): attended.reshape(LEADS, members, 2, channels)]
where the time goes in v3:
time: 65.3 us; the launch traced here: 65.1 us
  Pallas kernels  61.3 us (94%)
  local copies, waits for them, and re-layouts  3.14 us (5%)
    pallas_call x1, Pallas kernels, body(): pl.pallas_call(functools.partial(kernel, n_rows, n_cols, groups, members)...  61.3 us
    unnamed x7, local copies, waits for them, and re-layouts  3.14 us

profile of v3, /device:TPU:1, one launch (start us, length us, event | category | flops | bytes accessed | tf_op | source)
XLA Modules:
  0.0 65.1 jit_solution(4440449760275163560)
XLA Ops:
  0.6 61.3 %shard_map.130 = (bf16[1024,128]{1,0:T(8,128)(2,1)}, f32[1024,128]{1,0:T(8,128)}, f32[2,2,16,64]{3,2,1,0:T(8,128)}) custom-call(bf16[2,1024,128]{2,1,0:T(8,128)(2,1)} %bitcast.10, bf16[1024,128]{1,0:T(8,128)(2,1)} %bitcast.13, f32[1024,128]{1,0:T(8,128)} %bitcast.11, bf16[8,128,256]{2,1,0:T(8,128)(2,1)} %constant.4.clone.spread_ref, ...), custom_call_target="tpu_custom_call" | custom-call | tf_op jit(solution)/shard_map/pallas_call | solution.py:540
  61.9 0.0 copy-start
  62.0 1.7 %copy.17 = bf16[64,16,128]{2,1,0:T(8,128)(2,1)} copy(bf16[64,16,128]{2,1,0:T(8,128)(2,1)} %bitcast.14) | data formatting | bytes 524288
  63.7 0.0 copy-done
  63.7 0.0 copy-start.1
  63.7 0.8 %copy.18 = f32[64,16,128]{2,1,0:T(8,128)} copy(f32[64,16,128]{2,1,0:T(8,128)S(1)} %bitcast.12) | data formatting | bytes 1048576
  64.5 0.0 copy-done.1
  64.5 0.6 copy.19
Async XLA Ops:
  61.9 1.7 %copy-start = (f32[1024,128]{1,0:T(8,128)S(1)}, f32[1024,128]{1,0:T(8,128)}, u32[]{:S(2)}) copy-start(f32[1024,128]{1,0:T(8,128)} %get-tuple-element.7) | copy-start | bytes 1572868
  63.7 0.8 %copy-start.1 = (f32[2,2,16,64]{3,2,1,0:T(8,128)S(1)}, f32[2,2,16,64]{3,2,1,0:T(8,128)}, u32[]{:S(2)}) copy-start(f32[2,2,16,64]{3,2,1,0:T(8,128)} %get-tuple-element.8) | copy-start | bytes 49156

commit v4 on v3

--- a/solution.py
+++ b/solution.py
@@ -12,6 +12,7 @@
 LEADS = 2
 POOL = 8
 LINES = 4
+DEEP = 3
 MESH = pl.DeviceIdType.MESH
 F32 = jnp.float32
 BF16 = jnp.bfloat16
@@ -200,6 +201,8 @@
     recv_b,
     send_c,
     recv_c,
+    send_d,
+    recv_d,
 ):
     row, col = lax.axis_index("rows"), lax.axis_index("cols")
     core, group, line = row % 2, row // 2 % groups, row // (2 * groups)
@@ -215,8 +218,14 @@
         target = (member + step) % members
         return ((target // 2 * groups + group) * 2 + target % 2, col)
 
+    span = groups // DEEP
+    level, place_y = group // span, group % span
+
+    def upper(step):
+        return ((line * groups + (level + step) % DEEP * span + place_y) * 2 + core, col)
+
     def twin(step):
-        return ((line * groups + (group + step) % groups) * 2 + core, col)
+        return ((line * groups + level * span + (place_y + step) % span) * 2 + core, col)
 
     loads = [
         pltpu.make_async_copy(frames_ref.at[0], frames_in.at[0], local_sem.at[0]),
@@ -245,7 +254,8 @@
 
     barrier = pltpu.get_barrier_semaphore()
     peers = [near(dr, dc) for dr, dc in EDGE_WAYS] + [near(dr, 0) for dr in ROW_WAYS]
-    peers += [twin(step) for step in range(1, groups)] + [mate(step) for step in range(1, members)]
+    peers += [upper(step) for step in range(1, DEEP)] + [twin(step) for step in range(1, span)]
+    peers += [mate(step) for step in range(1, members)]
     for peer in peers:
         pl.semaphore_signal(barrier, inc=1, device_id=peer, device_id_type=MESH)
 
@@ -270,6 +280,12 @@
 
     pl.semaphore_wait(barrier, len(peers))
     sends = []
+
+    def settle(keep):
+        done = len(sends) - keep
+        for copy in sends[:done]:
+            copy.wait_send()
+        del sends[:done]
 
     def send(source, target, send_sem, recv_sem, device):
         copy = pltpu.make_async_remote_copy(
@@ -407,27 +423,39 @@
     def gather(lead, copies):
         for copy in copies:
             copy.wait_recv()
-        gathered[lead, group] = jnp.concatenate(
+        gathered[lead, place_y, level] = jnp.concatenate(
             [column[lead, :, k, :] for k in range(2)], axis=0
         ).astype(BF16)
-        copies = []
-        for step in range(1, groups):
-            copies.append(
-                send(
-                    gathered.at[lead, group],
-                    gathered.at[lead, group],
-                    send_b.at[lead, step],
-                    recv_b.at[lead, step],
-                    twin(step),
-                )
-            )
-        return copies
+        return [
+            send(
+                gathered.at[lead, place_y, level],
+                gathered.at[lead, place_y, level],
+                send_b.at[lead, step],
+                recv_b.at[lead, step],
+                upper(step),
+            )
+            for step in range(1, DEEP)
+        ]
+
+    def spread(lead, copies):
+        for copy in copies:
+            copy.wait_recv()
+        return [
+            send(
+                gathered.at[lead, place_y],
+                gathered.at[lead, place_y],
+                send_d.at[lead, step],
+                recv_d.at[lead, step],
+                twin(step),
+            )
+            for step in range(1, span)
+        ]
 
     def attend(lead, copies):
         for copy in copies:
             copy.wait_recv()
         attended = attend_column(
-            gathered[lead, group],
+            gathered[lead, place_y, level],
             gathered[lead].reshape(groups * 2 * members, both),
             mix,
             gain,
@@ -474,14 +502,18 @@
     update(1, spatial1)
     picked = dot_t(pick_in[:16, :], stacked[...])
     shared1 = share(1, picked)
+    spread0 = spread(0, gathered0)
+    settle(len(shared1) + len(spread0))
     store_cell = pltpu.make_async_copy(cell_now, cell_out, local_sem.at[6])
     store_cell.start()
     hidden_in[...] = plain[...].astype(BF16)
     store_hidden = pltpu.make_async_copy(hidden_in, hidden_out, local_sem.at[7])
     store_hidden.start()
-    returned0 = attend(0, gathered0)
     gathered1 = gather(1, shared1)
-    returned1 = attend(1, gathered1)
+    returned0 = attend(0, spread0)
+    spread1 = spread(1, gathered1)
+    settle(len(spread1))
+    returned1 = attend(1, spread1)
     for lead, copies in enumerate((returned0, returned1)):
         for copy in copies:
             copy.wait_recv()
@@ -490,8 +522,34 @@
             attended_out[lead, k] = attended[:, k * channels : (k + 1) * channels]
     store_cell.wait()
     store_hidden.wait()
-    for copy in sends:
-        copy.wait_send()
+    settle(0)
+
+
+def finish_kernel(*refs):
+    count = (len(refs) - 1) // 3
+    sources, targets, held, sem = refs[:count], refs[count : 2 * count], refs[2 * count : -1], refs[-1]
+    loads = [pltpu.make_async_copy(sources[k], held[k], sem.at[0, k]) for k in range(count)]
+    stores = [pltpu.make_async_copy(held[k], targets[k], sem.at[1, k]) for k in range(count)]
+    for load in loads:
+        load.start()
+    for load, store in zip(loads, stores):
+        load.wait()
+        store.start()
+    for store in stores:
+        store.wait()
+
+
+def finish(*arrays):
+    hbm = pl.BlockSpec(memory_space=pltpu.HBM)
+    return pl.pallas_call(
+        finish_kernel,
+        out_shape=tuple(jax.ShapeDtypeStruct(a.shape, a.dtype) for a in arrays),
+        in_specs=[hbm] * len(arrays),
+        out_specs=(hbm,) * len(arrays),
+        scratch_shapes=[pltpu.VMEM(a.shape, a.dtype) for a in arrays]
+        + [pltpu.SemaphoreType.DMA((2, len(arrays)))],
+        compiler_params=pltpu.CompilerParams(vmem_limit_bytes=60 * 2**20),
+    )(*arrays)
 
 
 def picker(cols):
@@ -578,7 +636,7 @@
             pltpu.VMEM((both, both), BF16),
             pltpu.VMEM((LEADS, members, 2, both), F32),
             pltpu.VMEM((LEADS, members, 2, both), F32),
-            pltpu.VMEM((LEADS, groups, 2 * members, both), BF16),
+            pltpu.VMEM((LEADS, groups // DEEP, DEEP, 2 * members, both), BF16),
             pltpu.VMEM((LEADS, members, 2, both), F32),
             pltpu.VMEM((LEADS, members, 2, both), F32),
             dma((15,)),
@@ -588,10 +646,12 @@
             dma((2, 6)),
             dma((LEADS, members)),
             dma((LEADS, members)),
-            dma((LEADS, groups)),
-            dma((LEADS, groups)),
+            dma((LEADS, DEEP)),
+            dma((LEADS, DEEP)),
             dma((LEADS, members)),
             dma((LEADS, members)),
+            dma((LEADS, groups // DEEP)),
+            dma((LEADS, groups // DEEP)),
         ],
         compiler_params=pltpu.CompilerParams(
             collective_id=0, has_side_effects=True, vmem_limit_bytes=60 * 2**20
@@ -609,6 +669,7 @@
         query_gain[None],
         output_weight,
     )
+    attended, cell, hidden = finish(attended, cell, hidden)
     attended = jnp.transpose(attended, (0, 3, 1, 2))
     shape = (channels, row_count, cols)
     return (hidden.reshape(shape), cell.reshape(shape), attended)

time: 65.3 us -> 60.5 us (0.926)
  local copies, waits for them, and re-layouts: 3.14 us -> 0 us
  Pallas kernels: 61.3 us -> 59.7 us
    pallas_call x1, Pallas kernels: 61.3 us -> 57.7 us  [body(): pl.pallas_call(functools.partial(kernel, n_rows, n_cols, groups, members)...]
    unnamed x7 -> x0, local copies, waits for them, and re-layouts: 3.14 us -> none
    pallas_call x0 -> x1, Pallas kernels: none -> 1.99 us  [finish(): pl.pallas_call(finish_kernel, out_shape=tuple((jax.ShapeDtypeStruct(a.sha...]
where the time goes in v4:
time: 60.5 us; the launch traced here: 60.3 us
  Pallas kernels  59.7 us (99%)
  between operations  0.64 us (1%)
    pallas_call x1, Pallas kernels, body(): pl.pallas_call(functools.partial(kernel, n_rows, n_cols, groups, members)...  57.7 us
    pallas_call x1, Pallas kernels, finish(): pl.pallas_call(finish_kernel, out_shape=tuple((jax.ShapeDtypeStruct(a.sha...  1.99 us

profile of v4, /device:TPU:1, one launch (start us, length us, event | category | flops | bytes accessed | tf_op | source)
XLA Modules:
  0.0 60.3 jit_solution(2018735268909442471)
XLA Ops:
  0.6 57.7 %shard_map.130 = (bf16[1024,128]{1,0:T(8,128)(2,1)}, f32[1024,128]{1,0:T(8,128)}, f32[2,2,16,64]{3,2,1,0:T(8,128)}) custom-call(bf16[2,1024,128]{2,1,0:T(8,128)(2,1)} %bitcast.10, bf16[1024,128]{1,0:T(8,128)(2,1)} %bitcast.12, f32[1024,128]{1,0:T(8,128)} %bitcast.11, bf16[8,128,256]{2,1,0:T(8,128)(2,1)} %constant.4.clone.spread_ref, ...), custom_call_target="tpu_custom_call" | custom-call | tf_op jit(solution)/shard_map/pallas_call | solution.py:598
  58.3 2.0 %shard_map.131 = (f32[2,2,16,64]{3,2,1,0:T(8,128)}, f32[1024,128]{1,0:T(8,128)}, bf16[1024,128]{1,0:T(8,128)(2,1)}) custom-call(f32[2,2,16,64]{3,2,1,0:T(8,128)} %get-tuple-element.9.refs_0_, f32[1024,128]{1,0:T(8,128)} %get-tuple-element.10.refs_1_, bf16[1024,128]{1,0:T(8,128)(2,1)} %get-tuple-element.11.refs_2_), custom_call_target="tpu_custom_call" | custom-call | tf_op jit(solution)/shard_map/pallas_call | solution.py:544

commit v5 on v4

--- a/solution.py
+++ b/solution.py
@@ -114,14 +114,14 @@
     lax.fori_loop(blocks[0], blocks[1], block, None)
 
 
-def halo_column(frame_tiles, hidden_tiles, way, masks, taps_t, pad_ref):
+def halo_column(frame_tiles, hidden_tiles, way, masks, taps_t, pad_ref, extra):
     seen, above, below = masks
     first = 8 if way == 1 else 0
     slot = {dr: EDGE_WAYS.index((dr, way)) for dr in (-1, 0, 1)}
 
     def part(dr):
         frame = frame_tiles(slot[dr]).astype(F32)[first : first + 8]
-        hidden = hidden_tiles(slot[dr]).astype(F32)[first : first + 8]
+        hidden = hidden_tiles(dr, way, first)
         low = lane_half(frame.shape)
         half = frame.shape[1] // 2
         upper = jnp.where(low, frame, pltpu.roll(hidden, half, 1))
@@ -134,7 +134,8 @@
     pad_ref[16:24] = lower
     pad_ref[24:32] = jnp.where(below, part(-1)[0], 0.0)
     b = 0 if way == 1 else 2
-    return sum(taps_t[3 * a + b] * pad_ref[7 + a : 23 + a] for a in range(3))
+    rows = [pad_ref[7 + a - extra : 23 + a + extra] for a in range(3)]
+    return sum(taps_t[3 * a + b] * rows[a] for a in range(3))
 
 
 def kernel(
@@ -174,12 +175,13 @@
     spatial1,
     weight,
     stacked,
-    row_out0,
-    row_in0,
+    row_out,
+    row_in,
+    cell_sent,
+    cell_rim,
     edge_out0,
     edge_in0,
-    row_out1,
-    row_in1,
+    stacked_rim,
     edge_out1,
     edge_in1,
     pad,
@@ -195,6 +197,8 @@
     recv_row,
     send_edge,
     recv_edge,
+    send_side,
+    recv_side,
     send_a,
     recv_a,
     send_b,
@@ -233,7 +237,7 @@
         pltpu.make_async_copy(frames_ref.at[1], frames_in.at[1], local_sem.at[2]),
         pltpu.make_async_copy(cell_ref, cell_now, local_sem.at[3]),
         pltpu.make_async_copy(spread_ref, spatial0.at[:, both:], local_sem.at[4]),
-        pltpu.make_async_copy(spread_ref, spatial1.at[:, both:], local_sem.at[5]),
+        pltpu.make_async_copy(spread_ref.at[:8], spatial1.at[:, both:], local_sem.at[5]),
     ]
     small = [
         pltpu.make_async_copy(source, target, local_sem.at[8 + k])
@@ -266,17 +270,22 @@
     ):
         load.wait()
         plain[...] = source[...].astype(F32)
-        target, base = ((x0, 0), (x0, channels), (x1, 0))[k]
+        target, base, first = ((x0, 0, 2), (x0, channels, 2), (x1, 0, 1))[k]
         for r in range(16):
             plane = plain[pl.ds(r, channels, stride=16), :]
-            target[r + 1, base : base + channels, :] = plane
+            target[r + first, base : base + channels, :] = plane
             low = plane.astype(BF16)
             stacked[
                 (r // 8) * channels : (r // 8 + 1) * channels, (r % 8) * cols : (r % 8 + 1) * cols
             ] = low
             if r in (0, 15):
-                row_out0[r // 15, k * channels : (k + 1) * channels, :] = low
+                row_out[r // 15, k * channels : (k + 1) * channels, :] = low
+            if r in (1, 14) and k < 2:
+                row_out[r // 14, (3 + k) * channels : (4 + k) * channels, :] = low
         edge_out0[k] = dot_t(pick_edges, stacked[...]).astype(BF16)
+    loads[3].wait()
+    for k, r in enumerate((0, 15)):
+        cell_sent[k] = cell_now[pl.ds(r, channels, stride=16), :]
 
     pl.semaphore_wait(barrier, len(peers))
     sends = []
@@ -300,31 +309,19 @@
         sends.append(copy)
         return copy
 
-    def send_halo(step, row_out, row_in, edge_out, edge_in):
-        copies = []
-        for k, dr in enumerate(ROW_WAYS):
-            copies.append(
-                send(
-                    row_out.at[k],
-                    row_in.at[k],
-                    send_row.at[step, k],
-                    recv_row.at[step, k],
-                    near(dr, 0),
-                )
-            )
-        for k, (dr, dc) in enumerate(EDGE_WAYS):
-            copies.append(
-                send(
-                    edge_out,
-                    edge_in.at[k],
-                    send_edge.at[step, k],
-                    recv_edge.at[step, k],
-                    near(dr, dc),
-                )
-            )
-        return copies
-
-    halo0 = send_halo(0, row_out0, row_in0, edge_out0, edge_in0)
+    row_copies, cell_copies, edge_copies = [], [], []
+    for k, (dr, dc) in enumerate(EDGE_WAYS):
+        edge_copies.append(
+            send(edge_out0, edge_in0.at[k], send_edge.at[k], recv_edge.at[k], near(dr, dc))
+        )
+    for k, dr in enumerate(ROW_WAYS):
+        row_copies.append(
+            send(row_out.at[k], row_in.at[k], send_row.at[0, k], recv_row.at[0, k], near(dr, 0))
+        )
+    for k, dr in enumerate(ROW_WAYS):
+        cell_copies.append(
+            send(cell_sent.at[k], cell_rim.at[k], send_row.at[1, k], recv_row.at[1, k], near(dr, 0))
+        )
 
     for load in small[1:]:
         load.wait()
@@ -339,66 +336,74 @@
     weight[:, :both] = (point_in[...].astype(F32) * halve).astype(BF16)
     for part in range(3):
         rounded = bias.astype(BF16).astype(F32)
-        bias_lanes = rounded if part == 0 else jnp.where(lane == 64 + part, rounded, bias_lanes)
+        bias_lanes = rounded if part == 0 else jnp.where(lane == 72 + part, rounded, bias_lanes)
         bias = bias - rounded
-    bias_lanes = jnp.where(lane < 67, bias_lanes, 0.0)
+    bias_lanes = jnp.where(lane < 75, bias_lanes, 0.0)
     mixing = jnp.transpose(mixing_in[...].astype(F32))
     for k in range(3):
         mix[k] = twice(mixing[k * channels : (k + 1) * channels]).astype(BF16)
     out_mix[...] = twice(output_in[...].astype(F32)).astype(BF16)
+    side_lane = lax.broadcasted_iota(jnp.int32, (16, cols), 1)
+    side_row = lax.broadcasted_iota(jnp.int32, (16, cols), 0)
+    pick_sides = jnp.where(
+        side_lane == side_row * (cols - 1), jnp.where(side_row < 2, 1.0, 0.0), 0.0
+    ).astype(BF16)
     gain = jnp.concatenate([gain_in[...], gain_in[...]], axis=1)
 
     above, below = row > 0, row < n_rows - 1
+    interior0, rim0 = ((2, 4), (6, 4), (10, 4), (14, 2)), ((0, 2), (16, 2))
     interior, rim = ((1, 4), (5, 4), (9, 4), (13, 2)), ((0, 1), (15, 1))
     whole = channels // 16
-    depthwise(x0, taps, spatial0, (0, 2 * whole), interior)
+    depthwise(x0, taps, spatial0, (0, 2 * whole), interior0)
     depthwise(x1, taps, spatial1, (0, whole), interior)
 
-    def fill_rows(x_ref, base, row_in, offset):
-        x_ref[0, base : base + channels, :] = jnp.where(
-            above, row_in[1, offset : offset + channels, :].astype(F32), 0.0
-        )
-        x_ref[17, base : base + channels, :] = jnp.where(
-            below, row_in[0, offset : offset + channels, :].astype(F32), 0.0
-        )
-
-    def extend(frame_tiles, hidden_tiles):
-        left = halo_column(frame_tiles, hidden_tiles, 1, (col > 0, above, below), taps_t, pad)
+    def fill_row(x_ref, place, base, valid, plane):
+        x_ref[place, base : base + channels, :] = jnp.where(valid, plane.astype(F32), 0.0)
+
+    def extend(frame_tiles, hidden_tiles, extra):
+        left = halo_column(
+            frame_tiles, hidden_tiles, 1, (col > 0, above, below), taps_t, pad, extra
+        )
         right = halo_column(
-            frame_tiles, hidden_tiles, -1, (col < n_cols - 1, above, below), taps_t, pad
-        )
-        rest = jnp.zeros((cols - 64, both), F32)
-        added = jnp.concatenate([left, right, left, right, rest], axis=0).astype(BF16)
+            frame_tiles, hidden_tiles, -1, (col < n_cols - 1, above, below), taps_t, pad, extra
+        )
+        short = jnp.zeros((2 - 2 * extra, both), F32)
+        added = [left, short, right, short] if extra == 0 else [left, right]
+        rest = jnp.zeros((cols - 72, both), F32)
+        added = jnp.concatenate(added + added + [rest], axis=0).astype(BF16)
         lifted = dot_t(weight[:, :both], added)
         rounded = lifted.astype(BF16).astype(F32)
         weight[:, both:] = jnp.where(
-            lane < 32, rounded, jnp.where(lane < 64, lifted - rounded, bias_lanes)
+            lane < 36, rounded, jnp.where(lane < 72, lifted - rounded, bias_lanes)
         ).astype(BF16)
 
     def update(step, spatial):
-        for pair in range(8):
+        for pair in range(9 - step):
             gates = dot(weight[...], spatial[pair])
             for j in range(2):
-                r = 2 * pair + j
+                r = 2 * pair + j - 1 + step
                 in_gate, forget, out_gate, candidate = (
                     jnp.tanh(gates[k * channels : (k + 1) * channels, j * cols : (j + 1) * cols])
                     for k in range(4)
                 )
+                outside = r < 0 or r > 15
                 place = pl.ds(r, channels, stride=16)
-                memory = (0.5 * forget + 0.5) * cell_now[place, :] + (
-                    0.5 * in_gate + 0.5
-                ) * candidate
-                cell_now[place, :] = memory
+                before = cell_rim[1 if r < 0 else 0] if outside else cell_now[place, :]
+                memory = (0.5 * forget + 0.5) * before + (0.5 * in_gate + 0.5) * candidate
                 hidden = (0.5 * out_gate + 0.5) * jnp.tanh(memory)
                 low = hidden.astype(BF16)
+                if outside:
+                    fill_row(x1, r + 1, channels, above if r < 0 else below, low)
+                    half = 1 if r < 0 else 0
+                    stacked_rim[half * channels : (half + 1) * channels, :] = low
+                    continue
+                cell_now[place, :] = memory
                 stacked[
                     (r // 8) * channels : (r // 8 + 1) * channels,
                     (r % 8) * cols : (r % 8 + 1) * cols,
                 ] = low
                 if step == 0:
                     x1[r + 1, channels:both, :] = low.astype(F32)
-                    if r in (0, 15):
-                        row_out1[r // 15] = low
                 else:
                     plain[place, :] = hidden
 
@@ -477,27 +482,48 @@
             )
         return copies
 
-    for copy in halo0:
+    def plane(k, index):
+        return row_in[k, index * channels : (index + 1) * channels, :]
+
+    def first_hidden(dr, way, first):
+        return edge_in0[EDGE_WAYS.index((dr, way)), 1].astype(F32)[first : first + 8]
+
+    def second_hidden(dr, way, first):
+        tile = edge_in1[0 if way == -1 else 1].astype(F32)
+        if dr == 0:
+            return tile[first : first + 8]
+        return jnp.broadcast_to(tile[16 + first // 8 : 17 + first // 8], (8, both))
+
+    for copy in edge_copies + row_copies:
         copy.wait_recv()
-    fill_rows(x0, 0, row_in0, 0)
-    fill_rows(x0, channels, row_in0, channels)
-    depthwise(x0, taps, spatial0, (0, 2 * whole), rim)
-    extend(lambda k: edge_in0[k, 0], lambda k: edge_in0[k, 1])
-    for load in loads[3:]:
+    for k in range(2):
+        fill_row(x0, 0, k * channels, above, plane(1, 3 + k))
+        fill_row(x0, 1, k * channels, above, plane(1, k))
+        fill_row(x0, 18, k * channels, below, plane(0, k))
+        fill_row(x0, 19, k * channels, below, plane(0, 3 + k))
+    depthwise(x0, taps, spatial0, (0, 2 * whole), rim0)
+    extend(lambda k: edge_in0[k, 0], first_hidden, 1)
+    for load in loads[4:]:
         load.wait()
+    for copy in cell_copies:
+        copy.wait_recv()
     update(0, spatial0)
     picked = dot_t(pick_in[...], stacked[...])
-    edge_out1[...] = picked[16:].astype(BF16)
-    halo1 = send_halo(1, row_out1, row_in1, edge_out1, edge_in1)
+    edge_out1[0:16] = picked[16:].astype(BF16)
+    edge_out1[16:32] = dot_t(pick_sides, stacked_rim[...]).astype(BF16)
+    side_copies = []
+    for k, dc in enumerate((-1, 1)):
+        side_copies.append(
+            send(edge_out1, edge_in1.at[k], send_side.at[k], recv_side.at[k], near(0, dc))
+        )
     shared0 = share(0, picked[:16])
-    fill_rows(x1, 0, row_in0, both)
+    fill_row(x1, 0, 0, above, plane(1, 2))
+    fill_row(x1, 17, 0, below, plane(0, 2))
     depthwise(x1, taps, spatial1, (0, whole), rim)
-    depthwise(x1, taps, spatial1, (whole, 2 * whole), interior)
-    for copy in halo1:
+    depthwise(x1, taps, spatial1, (whole, 2 * whole), interior + rim)
+    for copy in side_copies:
         copy.wait_recv()
-    fill_rows(x1, channels, row_in1, 0)
-    depthwise(x1, taps, spatial1, (whole, 2 * whole), rim)
-    extend(lambda k: edge_in0[k, 2], lambda k: edge_in1[k])
+    extend(lambda k: edge_in0[k, 2], second_hidden, 0)
     gathered0 = gather(0, shared0)
     update(1, spatial1)
     picked = dot_t(pick_in[:16, :], stacked[...])
@@ -563,15 +589,15 @@
 
 
 def spreader(cols):
-    spread = np.zeros((8, 128, 2, cols), np.float32)
-    for pair in range(8):
+    spread = np.zeros((9, 128, 2, cols), np.float32)
+    for pair in range(9):
         for j in range(2):
             r = 2 * pair + j
-            for twin in (0, 32):
+            for twin in (0, 36):
                 spread[pair, twin + r, j, 0] = 1.0
-                spread[pair, twin + 16 + r, j, cols - 1] = 1.0
-    spread[:, 64:67] = 1.0
-    return spread.reshape(8, 128, 2 * cols)
+                spread[pair, twin + 18 + r, j, cols - 1] = 1.0
+    spread[:, 72:75] = 1.0
+    return spread.reshape(9, 128, 2 * cols)
 
 
 def body(
@@ -616,21 +642,22 @@
             pltpu.VMEM((flat, cols), BF16),
             pltpu.VMEM((flat, cols), F32),
             pltpu.VMEM((flat, cols), F32),
-            pltpu.VMEM((row_count + 2, both, cols), F32),
+            pltpu.VMEM((row_count + 4, both, cols), F32),
             pltpu.VMEM((row_count + 2, both, cols), F32),
             pltpu.VMEM((9, both, cols), F32),
-            pltpu.VMEM((8, 2 * both, 2 * cols), BF16),
+            pltpu.VMEM((9, 2 * both, 2 * cols), BF16),
             pltpu.VMEM((8, 2 * both, 2 * cols), BF16),
             pltpu.VMEM((4 * channels, 2 * both), BF16),
             pltpu.VMEM((both, POOL * cols), BF16),
-            pltpu.VMEM((2, 3 * channels, cols), BF16),
-            pltpu.VMEM((2, 3 * channels, cols), BF16),
+            pltpu.VMEM((2, 5 * channels, cols), BF16),
+            pltpu.VMEM((2, 5 * channels, cols), BF16),
+            pltpu.VMEM((2, channels, cols), F32),
+            pltpu.VMEM((2, channels, cols), F32),
             pltpu.VMEM((3, 16, both), BF16),
             pltpu.VMEM((6, 3, 16, both), BF16),
-            pltpu.VMEM((2, channels, cols), BF16),
-            pltpu.VMEM((2, channels, cols), BF16),
-            pltpu.VMEM((16, both), BF16),
-            pltpu.VMEM((6, 16, both), BF16),
+            pltpu.VMEM((both, cols), BF16),
+            pltpu.VMEM((32, both), BF16),
+            pltpu.VMEM((2, 32, both), BF16),
             pltpu.VMEM((32, both), F32),
             pltpu.VMEM((3, both, both), BF16),
             pltpu.VMEM((both, both), BF16),
@@ -642,8 +669,10 @@
             dma((15,)),
             dma((2, 2)),
             dma((2, 2)),
-            dma((2, 6)),
-            dma((2, 6)),
+            dma((6,)),
+            dma((6,)),
+            dma((2,)),
+            dma((2,)),
             dma((LEADS, members)),
             dma((LEADS, members)),
             dma((LEADS, DEEP)),

time: 60.5 us -> 59.2 us (0.979)
  Pallas kernels: 59.7 us -> 58.4 us
    pallas_call x1, Pallas kernels: 57.7 us -> 56.4 us  [body(): pl.pallas_call(functools.partial(kernel, n_rows, n_cols, groups, members)...]
where the time goes in v5:
time: 59.2 us; the launch traced here: 59 us
  Pallas kernels  58.4 us (99%)
  between operations  0.64 us (1%)
    pallas_call x1, Pallas kernels, body(): pl.pallas_call(functools.partial(kernel, n_rows, n_cols, groups, members)...  56.4 us
    pallas_call x1, Pallas kernels, finish(): pl.pallas_call(finish_kernel, out_shape=tuple((jax.ShapeDtypeStruct(a.sha...  1.99 us

profile of v5, /device:TPU:1, one launch (start us, length us, event | category | flops | bytes accessed | tf_op | source)
XLA Modules:
  0.0 59.0 jit_solution(1780208658472785319)
XLA Ops:
  0.6 56.4 %shard_map.130 = (bf16[1024,128]{1,0:T(8,128)(2,1)}, f32[1024,128]{1,0:T(8,128)}, f32[2,2,16,64]{3,2,1,0:T(8,128)}) custom-call(bf16[2,1024,128]{2,1,0:T(8,128)(2,1)} %bitcast.10, bf16[1024,128]{1,0:T(8,128)(2,1)} %bitcast.12, f32[1024,128]{1,0:T(8,128)} %bitcast.11, bf16[9,128,256]{2,1,0:T(8,128)(2,1)} %constant.4.clone.spread_ref, ...), custom_call_target="tpu_custom_call" | custom-call | tf_op jit(solution)/shard_map/pallas_call | solution.py:624
  57.0 2.0 %shard_map.131 = (f32[2,2,16,64]{3,2,1,0:T(8,128)}, f32[1024,128]{1,0:T(8,128)}, bf16[1024,128]{1,0:T(8,128)(2,1)}) custom-call(f32[2,2,16,64]{3,2,1,0:T(8,128)} %get-tuple-element.9.refs_0_, f32[1024,128]{1,0:T(8,128)} %get-tuple-element.10.refs_1_, bf16[1024,128]{1,0:T(8,128)(2,1)} %get-tuple-element.11.refs_2_), custom_call_target="tpu_custom_call" | custom-call | tf_op jit(solution)/shard_map/pallas_call | solution.py:570

commit v6 on v5

--- a/solution.py
+++ b/solution.py
@@ -193,12 +193,8 @@
     result,
     returned,
     local_sem,
-    send_row,
-    recv_row,
-    send_edge,
-    recv_edge,
-    send_side,
-    recv_side,
+    halo_send,
+    halo_recv,
     send_a,
     recv_a,
     send_b,
@@ -292,9 +288,12 @@
 
     def settle(keep):
         done = len(sends) - keep
-        for copy in sends[:done]:
-            copy.wait_send()
+        for ref, sem in sends[:done]:
+            arrive(ref, sem)
         del sends[:done]
+
+    def arrive(ref, sem):
+        pltpu.make_async_copy(ref, ref, sem).wait()
 
     def send(source, target, send_sem, recv_sem, device):
         copy = pltpu.make_async_remote_copy(
@@ -306,22 +305,14 @@
             device_id_type=MESH,
         )
         copy.start()
-        sends.append(copy)
-        return copy
-
-    row_copies, cell_copies, edge_copies = [], [], []
+
     for k, (dr, dc) in enumerate(EDGE_WAYS):
-        edge_copies.append(
-            send(edge_out0, edge_in0.at[k], send_edge.at[k], recv_edge.at[k], near(dr, dc))
-        )
+        send(edge_out0, edge_in0.at[k], halo_send.at[0], halo_recv.at[0], near(dr, dc))
     for k, dr in enumerate(ROW_WAYS):
-        row_copies.append(
-            send(row_out.at[k], row_in.at[k], send_row.at[0, k], recv_row.at[0, k], near(dr, 0))
-        )
+        send(row_out.at[k], row_in.at[k], halo_send.at[1], halo_recv.at[1], near(dr, 0))
     for k, dr in enumerate(ROW_WAYS):
-        cell_copies.append(
-            send(cell_sent.at[k], cell_rim.at[k], send_row.at[1, k], recv_row.at[1, k], near(dr, 0))
-        )
+        send(cell_sent.at[k], cell_rim.at[k], halo_send.at[2], halo_recv.at[2], near(dr, 0))
+    sends += [(edge_in0, halo_send.at[0]), (row_out, halo_send.at[1]), (cell_sent, halo_send.at[2])]
 
     for load in small[1:]:
         load.wait()
@@ -412,53 +403,45 @@
         for k in range(members):
             given[lead, k] = pooled[2 * k : 2 * k + 2]
         column[lead, member] = given[lead, member]
-        copies = []
         for step in range(1, members):
-            copies.append(
-                send(
-                    given.at[lead, (member + step) % members],
-                    column.at[lead, member],
-                    send_a.at[lead, step],
-                    recv_a.at[lead, step],
-                    mate(step),
-                )
+            send(
+                given.at[lead, (member + step) % members],
+                column.at[lead, member],
+                send_a.at[lead],
+                recv_a.at[lead],
+                mate(step),
             )
-        return copies
-
-    def gather(lead, copies):
-        for copy in copies:
-            copy.wait_recv()
+        sends.append((given.at[lead, 1:], send_a.at[lead]))
+
+    def gather(lead):
+        arrive(column.at[lead, 1:], recv_a.at[lead])
         gathered[lead, place_y, level] = jnp.concatenate(
             [column[lead, :, k, :] for k in range(2)], axis=0
         ).astype(BF16)
-        return [
+        for step in range(1, DEEP):
             send(
                 gathered.at[lead, place_y, level],
                 gathered.at[lead, place_y, level],
-                send_b.at[lead, step],
-                recv_b.at[lead, step],
+                send_b.at[lead],
+                recv_b.at[lead],
                 upper(step),
             )
-            for step in range(1, DEEP)
-        ]
-
-    def spread(lead, copies):
-        for copy in copies:
-            copy.wait_recv()
-        return [
+        sends.append((gathered.at[lead, 0, 1:], send_b.at[lead]))
+
+    def spread(lead):
+        arrive(gathered.at[lead, 0, 1:], recv_b.at[lead])
+        for step in range(1, span):
             send(
                 gathered.at[lead, place_y],
                 gathered.at[lead, place_y],
-                send_d.at[lead, step],
-                recv_d.at[lead, step],
+                send_d.at[lead],
+                recv_d.at[lead],
                 twin(step),
             )
-            for step in range(1, span)
-        ]
-
-    def attend(lead, copies):
-        for copy in copies:
-            copy.wait_recv()
+        sends.append((gathered.at[lead, 1:], send_d.at[lead]))
+
+    def attend(lead):
+        arrive(gathered.at[lead, 1:], recv_d.at[lead])
         attended = attend_column(
             gathered[lead, place_y, level],
             gathered[lead].reshape(groups * 2 * members, both),
@@ -469,18 +452,15 @@
         for k in range(2):
             result[lead, :, k, :] = attended[k * members : (k + 1) * members]
         returned[lead, member] = result[lead, member]
-        copies = []
         for step in range(1, members):
-            copies.append(
-                send(
-                    result.at[lead, (member + step) % members],
-                    returned.at[lead, member],
-                    send_c.at[lead, step],
-                    recv_c.at[lead, step],
-                    mate(step),
-                )
+            send(
+                result.at[lead, (member + step) % members],
+                returned.at[lead, member],
+                send_c.at[lead],
+                recv_c.at[lead],
+                mate(step),
             )
-        return copies
+        sends.append((result.at[lead, 1:], send_c.at[lead]))
 
     def plane(k, index):
         return row_in[k, index * channels : (index + 1) * channels, :]
@@ -494,8 +474,8 @@
             return tile[first : first + 8]
         return jnp.broadcast_to(tile[16 + first // 8 : 17 + first // 8], (8, both))
 
-    for copy in edge_copies + row_copies:
-        copy.wait_recv()
+    arrive(edge_in0, halo_recv.at[0])
+    arrive(row_in, halo_recv.at[1])
     for k in range(2):
         fill_row(x0, 0, k * channels, above, plane(1, 3 + k))
         fill_row(x0, 1, k * channels, above, plane(1, k))
@@ -505,44 +485,39 @@
     extend(lambda k: edge_in0[k, 0], first_hidden, 1)
     for load in loads[4:]:
         load.wait()
-    for copy in cell_copies:
-        copy.wait_recv()
+    arrive(cell_rim, halo_recv.at[2])
     update(0, spatial0)
     picked = dot_t(pick_in[...], stacked[...])
     edge_out1[0:16] = picked[16:].astype(BF16)
     edge_out1[16:32] = dot_t(pick_sides, stacked_rim[...]).astype(BF16)
-    side_copies = []
     for k, dc in enumerate((-1, 1)):
-        side_copies.append(
-            send(edge_out1, edge_in1.at[k], send_side.at[k], recv_side.at[k], near(0, dc))
-        )
-    shared0 = share(0, picked[:16])
+        send(edge_out1, edge_in1.at[k], halo_send.at[3], halo_recv.at[3], near(0, dc))
+    sends.append((edge_in1, halo_send.at[3]))
+    share(0, picked[:16])
     fill_row(x1, 0, 0, above, plane(1, 2))
     fill_row(x1, 17, 0, below, plane(0, 2))
     depthwise(x1, taps, spatial1, (0, whole), rim)
     depthwise(x1, taps, spatial1, (whole, 2 * whole), interior + rim)
-    for copy in side_copies:
-        copy.wait_recv()
+    arrive(edge_in1, halo_recv.at[3])
     extend(lambda k: edge_in0[k, 2], second_hidden, 0)
-    gathered0 = gather(0, shared0)
     update(1, spatial1)
     picked = dot_t(pick_in[:16, :], stacked[...])
-    shared1 = share(1, picked)
-    spread0 = spread(0, gathered0)
-    settle(len(shared1) + len(spread0))
+    share(1, picked)
+    gather(0)
+    settle(2)
     store_cell = pltpu.make_async_copy(cell_now, cell_out, local_sem.at[6])
     store_cell.start()
     hidden_in[...] = plain[...].astype(BF16)
     store_hidden = pltpu.make_async_copy(hidden_in, hidden_out, local_sem.at[7])
     store_hidden.start()
-    gathered1 = gather(1, shared1)
-    returned0 = attend(0, spread0)
-    spread1 = spread(1, gathered1)
-    settle(len(spread1))
-    returned1 = attend(1, spread1)
-    for lead, copies in enumerate((returned0, returned1)):
-        for copy in copies:
-            copy.wait_recv()
+    gather(1)
+    spread(0)
+    spread(1)
+    attend(0)
+    settle(2)
+    attend(1)
+    for lead in range(LEADS):
+        arrive(returned.at[lead, 1:], recv_c.at[lead])
         attended = jnp.concatenate([returned[lead, k] for k in range(members)], axis=0)
         for k in range(2):
             attended_out[lead, k] = attended[:, k * channels : (k + 1) * channels]
@@ -667,20 +642,16 @@
             pltpu.VMEM((LEADS, members, 2, both), F32),
             pltpu.VMEM((LEADS, members, 2, both), F32),
             dma((15,)),
-            dma((2, 2)),
-            dma((2, 2)),
-            dma((6,)),
-            dma((6,)),
-            dma((2,)),
-            dma((2,)),
-            dma((LEADS, members)),
-            dma((LEADS, members)),
-            dma((LEADS, DEEP)),
-            dma((LEADS, DEEP)),
-            dma((LEADS, members)),
-            dma((LEADS, members)),
-            dma((LEADS, groups // DEEP)),
-            dma((LEADS, groups // DEEP)),
+            dma((4,)),
+            dma((4,)),
+            dma((LEADS,)),
+            dma((LEADS,)),
+            dma((LEADS,)),
+            dma((LEADS,)),
+            dma((LEADS,)),
+            dma((LEADS,)),
+            dma((LEADS,)),
+            dma((LEADS,)),
         ],
         compiler_params=pltpu.CompilerParams(
             collective_id=0, has_side_effects=True, vmem_limit_bytes=60 * 2**20

time: 59.2 us -> 55.2 us (0.932)
  Pallas kernels: 58.4 us -> 54.4 us
    pallas_call x1, Pallas kernels: 56.4 us -> 52.4 us  [body(): pl.pallas_call(functools.partial(kernel, n_rows, n_cols, groups, members)...]
where the time goes in v6:
time: 55.2 us; the launch traced here: 55.1 us
  Pallas kernels  54.4 us (99%)
  between operations  0.64 us (1%)
    pallas_call x1, Pallas kernels, body(): pl.pallas_call(functools.partial(kernel, n_rows, n_cols, groups, members)...  52.4 us
    pallas_call x1, Pallas kernels, finish(): pl.pallas_call(finish_kernel, out_shape=tuple((jax.ShapeDtypeStruct(a.sha...  1.99 us

profile of v6, /device:TPU:1, one launch (start us, length us, event | category | flops | bytes accessed | tf_op | source)
XLA Modules:
  0.0 55.1 jit_solution(1885254824150273929)
XLA Ops:
  0.6 52.4 %shard_map.130 = (bf16[1024,128]{1,0:T(8,128)(2,1)}, f32[1024,128]{1,0:T(8,128)}, f32[2,2,16,64]{3,2,1,0:T(8,128)}) custom-call(bf16[2,1024,128]{2,1,0:T(8,128)(2,1)} %bitcast.10, bf16[1024,128]{1,0:T(8,128)(2,1)} %bitcast.12, f32[1024,128]{1,0:T(8,128)} %bitcast.11, bf16[9,128,256]{2,1,0:T(8,128)(2,1)} %constant.4.clone.spread_ref, ...), custom_call_target="tpu_custom_call" | custom-call | tf_op jit(solution)/shard_map/pallas_call | solution.py:599
  53.1 2.0 %shard_map.131 = (f32[2,2,16,64]{3,2,1,0:T(8,128)}, f32[1024,128]{1,0:T(8,128)}, bf16[1024,128]{1,0:T(8,128)(2,1)}) custom-call(f32[2,2,16,64]{3,2,1,0:T(8,128)} %get-tuple-element.9.refs_0_, f32[1024,128]{1,0:T(8,128)} %get-tuple-element.10.refs_1_, bf16[1024,128]{1,0:T(8,128)(2,1)} %get-tuple-element.11.refs_2_), custom_call_target="tpu_custom_call" | custom-call | tf_op jit(solution)/shard_map/pallas_call | solution.py:545
